TPU v7x, 128 devices: a whole 4x4x4 slice. The times are simulated.
128 devices in a mesh: lat: 8 (over x, y_lo), lon: 16 (over y_hi, z, core).
Axes of the slice: x: 4, y: 4 (y_hi: 2, y_lo: 2; y = y_hi * 2 + y_lo), z: 4, core: 2. Of those that a mesh axis runs over, the one named last changes fastest.
Arguments:
- innovations: float32 [25, 65536], P(None, ('lat', 'lon')), may hold values from -6 to 6
- owners: int32 [65536, 1], P(('lat', 'lon')), may hold values from 0 to 127, as said below
- prof_row: int32 [65536], P(('lat', 'lon')), may hold values from 0 to 254
- prof_col: int32 [65536], P(('lat', 'lon')), may hold values from 0 to 126
- interp_weights: float32 [4, 65536], P(None, ('lat', 'lon')), may hold values from 0.1 to 1
- model_tiles: float32 [25, 4096, 8, 128], P(None, ('lat', 'lon')), may hold values from -6 to 6
- model_ids: int32 [1, 4096], P(None, ('lat', 'lon')), may hold values from 0 to 31, as said below
- face_x: float32 [2048, 2048], P('lat', 'lon'), may hold values from 0.02 to 0.12
- face_y: float32 [2048, 2048], P('lat', 'lon'), may hold values from 0.02 to 0.12
- cross_term: float32 [2048, 2048], P('lat', 'lon'), may hold values from -0.08 to 0.08
- wet_mask: int32 [2048, 2048], P('lat', 'lon'), may hold values 0 or 1
- norm_factor: float32 [25, 2048, 2048], P(None, 'lat', 'lon'), may hold values from 0.4 to 2.5
Outputs:
- smoothed: float32 [25, 2048, 2048], P(None, 'lat', 'lon')
- profile_values: float32 [25, 65536], P(None, ('lat', 'lon'))
Inputs may be any that keep to these rules, and one draw needn't show every extreme that they name: `owners`: among the 512 profiles of one device no owner appears more than 8 times; in every draw one owner appears exactly 8 times among every device's profiles. Owners count analysis blocks in lat-major order. `model_ids`: the 32 slots of the model device at lat index i and lon index g form as many equal groups as the lon axis has devices; group j holds tiles of the analysis block at lat index i and lon index j, and every analysis block's 32 tiles appear exactly once over its lat row.
All inputs are finite; a program needn't handle non-finite values. No bound on the sum of `wet_mask` on one device may be relied on, other than what follows from the above.
Results may differ from a plain program's by a relative error of at most 0.00002.
Values sent between devices are 32-bit elements; how exact they have to be, the bound alone decides.
A program may use at most 128 MiB of HBM per device.

v0:
```python
import jax
import jax.numpy as jnp
from jax import lax
from jax.sharding import PartitionSpec as P

STEPS = 10


def with_halo(cells, sides, width, closed):
    for axis, dim in sides:
        count = lax.axis_size(axis)
        ends = count if closed else count - 1
        head = lax.slice_in_dim(cells, 0, width, axis=dim)
        tail = lax.slice_in_dim(cells, cells.shape[dim] - width, cells.shape[dim], axis=dim)
        cells = jnp.concatenate(
            [
                lax.ppermute(tail, axis, [(i, (i + 1) % count) for i in range(ends)]),
                cells,
                lax.ppermute(head, axis, [((i + 1) % count, i) for i in range(ends)]),
            ],
            axis=dim,
        )
    return cells


def rims(values, width):
    widened = with_halo(values, (("lon", 2),), width, True)
    return with_halo(widened, (("lat", 1),), width, False)


def face_weights(stack):
    face_east = stack[0]
    face_north = stack[1]
    twist_field = stack[2]
    wet_cells = stack[3]
    east_face = face_east[1:-1, 1:-1] * wet_cells[1:-1, 1:-1] * wet_cells[1:-1, 2:]
    west_face = face_east[1:-1, :-2] * wet_cells[1:-1, :-2] * wet_cells[1:-1, 1:-1]
    north_face = face_north[1:-1, 1:-1] * wet_cells[1:-1, 1:-1] * wet_cells[2:, 1:-1]
    south_face = face_north[:-2, 1:-1] * wet_cells[:-2, 1:-1] * wet_cells[1:-1, 1:-1]
    twist_face = twist_field[1:-1, 1:-1] * wet_cells[1:-1, 1:-1]
    return (east_face, west_face, north_face, south_face, twist_face)


def trimmed(weights, offset):
    height = weights[0].shape[0]
    across = weights[0].shape[1]
    return tuple(
        (weight[offset : height - offset, offset : across - offset][None] for weight in weights)
    )


def advance(padded, sectioned):
    east_face, west_face, north_face, south_face, twist_face = sectioned
    centre = padded[:, 1:-1, 1:-1]
    return (
        centre
        + east_face * (padded[:, 1:-1, 2:] - centre)
        + west_face * (padded[:, 1:-1, :-2] - centre)
        + north_face * (padded[:, 2:, 1:-1] - centre)
        + south_face * (padded[:, :-2, 1:-1] - centre)
        + 0.25
        * twist_face
        * (padded[:, 2:, 2:] - padded[:, 2:, :-2] - padded[:, :-2, 2:] + padded[:, :-2, :-2])
    )


def on_device(
    innovations,
    owners,
    prof_row,
    prof_col,
    interp_weights,
    model_tiles,
    model_ids,
    face_x,
    face_y,
    cross_term,
    wet_mask,
    norm_factor,
):
    levels = norm_factor.shape[0]
    lat_cells = norm_factor.shape[1]
    lon_cells = norm_factor.shape[2]
    moved_tiles, moved_ids = (
        lax.all_to_all(model_tiles, "lon", split_axis=1, concat_axis=1, tiled=True),
        lax.all_to_all(model_ids, "lon", split_axis=1, concat_axis=1, tiled=True),
    )
    increment = jnp.zeros_like(moved_tiles).at[:, moved_ids[0]].set(moved_tiles)
    increment = increment.reshape(levels, lat_cells, lon_cells)
    devices = lax.axis_size(("lat", "lon"))
    local_count = innovations.shape[1]
    capacity = 2 * local_count // devices
    owner_list = owners[:, 0]
    one_hot = (owner_list[:, None] == jnp.arange(devices, dtype=jnp.int32)[None, :]).astype(
        jnp.int32
    )
    running = jnp.cumsum(one_hot, axis=0)
    rank_in = jnp.sum(running * one_hot, axis=1) - 1
    slot_of = owner_list * capacity + rank_in
    payload = jnp.concatenate([innovations, interp_weights], axis=0)
    send_float = (
        jnp.zeros((levels + 4, devices * capacity), jnp.float32).at[:, slot_of].set(payload)
    )
    location = prof_row * lon_cells + prof_col
    send_index = jnp.zeros((1, devices * capacity), jnp.int32).at[0, slot_of].set(location)
    recv_float, recv_index = (
        lax.all_to_all(send_float, ("lat", "lon"), split_axis=1, concat_axis=1, tiled=True),
        lax.all_to_all(send_index, ("lat", "lon"), split_axis=1, concat_axis=1, tiled=True),
    )
    base_cell = recv_index[0]
    recv_values = recv_float[:levels]
    recv_weights = recv_float[levels:]
    corner_cells = jnp.concatenate(
        [base_cell, base_cell + 1, base_cell + lon_cells, base_cell + lon_cells + 1]
    )
    spread = jnp.concatenate(
        [recv_values * recv_weights[corner][None, :] for corner in range(4)], axis=1
    )
    observed = (
        jnp.zeros((levels, lat_cells * lon_cells), jnp.float32).at[:, corner_cells].add(spread)
    )
    observed = observed.reshape(levels, lat_cells, lon_cells)
    field = norm_factor * (observed + increment)
    depth = 1
    stacked = jnp.stack([face_x, face_y, cross_term, wet_mask.astype(jnp.float32)])
    weights = face_weights(rims(stacked, depth + 1))
    sectioned_list = [trimmed(weights, 1)]

    def sweep(number, values):
        padded = rims(values, depth)
        padded = advance(padded, sectioned_list[0])
        return padded

    field = lax.fori_loop(0, STEPS // depth, sweep, field)
    smoothed = norm_factor * field
    flat_field = smoothed.reshape(levels, -1)
    sampled = (
        recv_weights[0][None, :] * flat_field[:, base_cell]
        + recv_weights[1][None, :] * flat_field[:, base_cell + 1]
        + recv_weights[2][None, :] * flat_field[:, base_cell + lon_cells]
        + recv_weights[3][None, :] * flat_field[:, base_cell + lon_cells + 1]
    )
    returned = lax.all_to_all(sampled, ("lat", "lon"), split_axis=1, concat_axis=1, tiled=True)
    profile_values = returned[:, slot_of]
    return (smoothed, profile_values)


def solution(mesh):
    in_specs = (
        P(None, ("lat", "lon")),
        P(("lat", "lon"), None),
        P(("lat", "lon")),
        P(("lat", "lon")),
        P(None, ("lat", "lon")),
        P(None, ("lat", "lon"), None, None),
        P(None, ("lat", "lon")),
        P("lat", "lon"),
        P("lat", "lon"),
        P("lat", "lon"),
        P("lat", "lon"),
        P(None, "lat", "lon"),
    )
    out_specs = (P(None, "lat", "lon"), P(None, ("lat", "lon")))
    return jax.shard_map(
        on_device, mesh=mesh, in_specs=in_specs, out_specs=out_specs, check_vma=False
    )
```

profile of v0, /device:TPU:1, one launch (start us, length us, event | category | flops | bytes accessed | tf_op | source)
XLA Modules:
  0.0 929.4 jit_solution(13546743064360122939)
XLA Ops:
  3.3 9.5 %all-to-all-start.2 = ((s32[1,16,2]{2,0,1:T(1,128)}), s32[1,16,2]{2,0,1:T(1,128)}, u32[]{:S(2)}, u32[]{:S(2)}) async-start(s32[1,16,2]{2,0,1:T(1,128)} %bitcast.19), calls=%async_computation.2 | async-start | bytes 16384 | tf_op jit(solution)/shard_map/all_to_all | solution.py:86
  26.9 4.0 copy.123
  34.0 10.6 %all-to-all-start = ((s32[1,128,8]{2,0,1:T(1,128)}), s32[1,128,8]{2,0,1:T(1,128)S(1)}, u32[]{:S(2)}, u32[]{:S(2)}) async-start(s32[1,128,8]{2,0,1:T(1,128)} %bitcast.170), calls=%async_computation | async-start | bytes 131072 | tf_op jit(solution)/shard_map/all_to_all | solution.py:108
  46.6 7.7 all-to-all-done
  54.3 4.3 all-to-all-start.1
  60.5 8.2 all-to-all-done.1
  68.7 4.6 all-to-all-start.3
  79.1 44.3 %collective-permute-done.6 = f32[4,2,132]{1,2,0:T(8,128)S(1)} collective-permute-done((f32[4,2,132]{1,2,0:T(8,128)S(1)}, f32[4,2,132]{1,2,0:T(8,128)S(1)}, u32[]{:S(2)}, u32[]{:S(2)}) %collective-permute-start.6) | collective-permute-done | bytes 4256 | tf_op jit(solution)/shard_map/ppermute | solution.py:17
  137.0 29.1 %scatter_custom_fusion.2 = f32[25,32768]{0,1:T(8,128)} fusion(s32[4096]{0:T(1024)S(1)} %bitcast.174, f32[4096,25]{1,0:T(8,128)S(1)} %copy.121, f32[]{:T(128)} %constant.8.clone.1), kind=kCustom, calls=%fused_computation.34 | custom fusion | flops 102400 | bytes 3276804 | tf_op jit(solution)/shard_map/scatter-add | solution.py:120
  166.1 13.8 %copy.124 = f32[25,256,128]{1,2,0:T(8,128)} copy(f32[25,256,128]{0,2,1:T(8,128)} %bitcast.142) | data formatting | bytes 6553600 | tf_op jit(solution)/shard_map/reshape | solution.py:122
  180.5 5.0 scatter_fusion
  188.7 4.6 add_multiply_fusion
  193.2 662.8 %while.10 = (s32[]{:T(128)}, f32[25,256,128]{1,2,0:T(8,128)S(1)}, f32[1,256,128]{1,2,0:T(8,128)}, f32[1,256,128]{1,2,0:T(8,128)S(1)}, f32[1,256,128]{1,2,0:T(8,1...) while((s32[]{:T(128)}, f32[25,256,128]{1,2,0:T(8,128)S(1)}, ...), condition=%wide.region_8.9_spmd, body=%wide.region_7.8_spmd.sunk | while | flops 20622068 | bytes 71233680 | solution.py:134
  194.3 6.1 collective-permute-start.1
  200.4 3.7 copy.160
  213.2 5.4 collective-permute-start.3
  225.3 14.4 %pad_maximum_fusion.15 = (f32[25,257,130]{2,1,0:T(8,128)}, f32[25,257,130]{2,1,0:T(8,128)}) fusion(f32[25,1,130]{2,1,0:T(1,128)} %collective-permute-done.2, f32[25,256,1]{2,1,0:T(8,128)} %copy.159, f32[25,256,128]{2,1,0:T(8,128)S(1)} %copy.160, f32[25,256,1]{2,1,0:T(8,128)} %copy.161, f32[25,1,130]{2,1,0:T(1,128)} %collective-permute-done.3), kind=kLoop, calls=%fused_computation.9.clone.1 | loop fusion | flops 5011500 | bytes 10036000 | tf_op jit(solution)/shard_map/while/body/eval_jaxpr/concatenate | solution.py:15
  239.7 17.5 %fusion.46 = f32[25,256,128]{2,1,0:T(8,128)} fusion(f32[25,257,130]{2,1,0:T(8,128)} %get-tuple-element.182, f32[25,257,130]{2,1,0:T(8,128)} %get-tuple-element.183, f32[25,256,128]{2,1,0:T(8,128)S(1)} %copy.160, f32[25,256,1]{2,1,0:T(8,128)} %copy.161, f32[25,256,1]{2,1,0:T(8,128)} %copy.159, f32[256,128]{1,0:T(8,128)} %copy.162, ...), kind=kLoop, calls=%fused_computation.13.clone.1 | loop fusion | flops 15564800 | bytes 26920960 | tf_op jit(solution)/shard_map/while/body/eval_jaxpr/add | solution.py:56
  263.6 3.7 copy.160
  276.4 5.2 collective-permute-start.3
  288.3 14.4 %pad_maximum_fusion.15 = (f32[25,257,130]{2,1,0:T(8,128)}, f32[25,257,130]{2,1,0:T(8,128)}) fusion(f32[25,1,130]{2,1,0:T(1,128)} %collective-permute-done.2, f32[25,256,1]{2,1,0:T(8,128)} %copy.159, f32[25,256,128]{2,1,0:T(8,128)S(1)} %copy.160, f32[25,256,1]{2,1,0:T(8,128)} %copy.161, f32[25,1,130]{2,1,0:T(1,128)} %collective-permute-done.3), kind=kLoop, calls=%fused_computation.9.clone.1 | loop fusion | flops 5011500 | bytes 10036000 | tf_op jit(solution)/shard_map/while/body/eval_jaxpr/concatenate | solution.py:15
  302.7 17.5 %fusion.46 = f32[25,256,128]{2,1,0:T(8,128)} fusion(f32[25,257,130]{2,1,0:T(8,128)} %get-tuple-element.182, f32[25,257,130]{2,1,0:T(8,128)} %get-tuple-element.183, f32[25,256,128]{2,1,0:T(8,128)S(1)} %copy.160, f32[25,256,1]{2,1,0:T(8,128)} %copy.161, f32[25,256,1]{2,1,0:T(8,128)} %copy.159, f32[256,128]{1,0:T(8,128)} %copy.162, ...), kind=kLoop, calls=%fused_computation.13.clone.1 | loop fusion | flops 15564800 | bytes 26920960 | tf_op jit(solution)/shard_map/while/body/eval_jaxpr/add | solution.py:56
  329.4 3.7 copy.160
  342.2 5.2 collective-permute-start.3
  354.1 14.4 %pad_maximum_fusion.15 = (f32[25,257,130]{2,1,0:T(8,128)}, f32[25,257,130]{2,1,0:T(8,128)}) fusion(f32[25,1,130]{2,1,0:T(1,128)} %collective-permute-done.2, f32[25,256,1]{2,1,0:T(8,128)} %copy.159, f32[25,256,128]{2,1,0:T(8,128)S(1)} %copy.160, f32[25,256,1]{2,1,0:T(8,128)} %copy.161, f32[25,1,130]{2,1,0:T(1,128)} %collective-permute-done.3), kind=kLoop, calls=%fused_computation.9.clone.1 | loop fusion | flops 5011500 | bytes 10036000 | tf_op jit(solution)/shard_map/while/body/eval_jaxpr/concatenate | solution.py:15
  368.5 17.5 %fusion.46 = f32[25,256,128]{2,1,0:T(8,128)} fusion(f32[25,257,130]{2,1,0:T(8,128)} %get-tuple-element.182, f32[25,257,130]{2,1,0:T(8,128)} %get-tuple-element.183, f32[25,256,128]{2,1,0:T(8,128)S(1)} %copy.160, f32[25,256,1]{2,1,0:T(8,128)} %copy.161, f32[25,256,1]{2,1,0:T(8,128)} %copy.159, f32[256,128]{1,0:T(8,128)} %copy.162, ...), kind=kLoop, calls=%fused_computation.13.clone.1 | loop fusion | flops 15564800 | bytes 26920960 | tf_op jit(solution)/shard_map/while/body/eval_jaxpr/add | solution.py:56
  391.3 4.7 collective-permute-start
  396.0 3.7 copy.160
  408.8 5.2 collective-permute-start.3
  420.7 14.4 %pad_maximum_fusion.15 = (f32[25,257,130]{2,1,0:T(8,128)}, f32[25,257,130]{2,1,0:T(8,128)}) fusion(f32[25,1,130]{2,1,0:T(1,128)} %collective-permute-done.2, f32[25,256,1]{2,1,0:T(8,128)} %copy.159, f32[25,256,128]{2,1,0:T(8,128)S(1)} %copy.160, f32[25,256,1]{2,1,0:T(8,128)} %copy.161, f32[25,1,130]{2,1,0:T(1,128)} %collective-permute-done.3), kind=kLoop, calls=%fused_computation.9.clone.1 | loop fusion | flops 5011500 | bytes 10036000 | tf_op jit(solution)/shard_map/while/body/eval_jaxpr/concatenate | solution.py:15
  435.1 17.5 %fusion.46 = f32[25,256,128]{2,1,0:T(8,128)} fusion(f32[25,257,130]{2,1,0:T(8,128)} %get-tuple-element.182, f32[25,257,130]{2,1,0:T(8,128)} %get-tuple-element.183, f32[25,256,128]{2,1,0:T(8,128)S(1)} %copy.160, f32[25,256,1]{2,1,0:T(8,128)} %copy.161, f32[25,256,1]{2,1,0:T(8,128)} %copy.159, f32[256,128]{1,0:T(8,128)} %copy.162, ...), kind=kLoop, calls=%fused_computation.13.clone.1 | loop fusion | flops 15564800 | bytes 26920960 | tf_op jit(solution)/shard_map/while/body/eval_jaxpr/add | solution.py:56
  457.9 4.7 collective-permute-start
  462.6 3.7 copy.160
  475.5 5.2 collective-permute-start.3
  487.4 14.4 %pad_maximum_fusion.15 = (f32[25,257,130]{2,1,0:T(8,128)}, f32[25,257,130]{2,1,0:T(8,128)}) fusion(f32[25,1,130]{2,1,0:T(1,128)} %collective-permute-done.2, f32[25,256,1]{2,1,0:T(8,128)} %copy.159, f32[25,256,128]{2,1,0:T(8,128)S(1)} %copy.160, f32[25,256,1]{2,1,0:T(8,128)} %copy.161, f32[25,1,130]{2,1,0:T(1,128)} %collective-permute-done.3), kind=kLoop, calls=%fused_computation.9.clone.1 | loop fusion | flops 5011500 | bytes 10036000 | tf_op jit(solution)/shard_map/while/body/eval_jaxpr/concatenate | solution.py:15
  501.8 17.5 %fusion.46 = f32[25,256,128]{2,1,0:T(8,128)} fusion(f32[25,257,130]{2,1,0:T(8,128)} %get-tuple-element.182, f32[25,257,130]{2,1,0:T(8,128)} %get-tuple-element.183, f32[25,256,128]{2,1,0:T(8,128)S(1)} %copy.160, f32[25,256,1]{2,1,0:T(8,128)} %copy.161, f32[25,256,1]{2,1,0:T(8,128)} %copy.159, f32[256,128]{1,0:T(8,128)} %copy.162, ...), kind=kLoop, calls=%fused_computation.13.clone.1 | loop fusion | flops 15564800 | bytes 26920960 | tf_op jit(solution)/shard_map/while/body/eval_jaxpr/add | solution.py:56
  524.6 4.7 collective-permute-start
  529.3 3.7 copy.160
  542.1 5.2 collective-permute-start.3
  554.0 14.4 %pad_maximum_fusion.15 = (f32[25,257,130]{2,1,0:T(8,128)}, f32[25,257,130]{2,1,0:T(8,128)}) fusion(f32[25,1,130]{2,1,0:T(1,128)} %collective-permute-done.2, f32[25,256,1]{2,1,0:T(8,128)} %copy.159, f32[25,256,128]{2,1,0:T(8,128)S(1)} %copy.160, f32[25,256,1]{2,1,0:T(8,128)} %copy.161, f32[25,1,130]{2,1,0:T(1,128)} %collective-permute-done.3), kind=kLoop, calls=%fused_computation.9.clone.1 | loop fusion | flops 5011500 | bytes 10036000 | tf_op jit(solution)/shard_map/while/body/eval_jaxpr/concatenate | solution.py:15
  568.4 17.5 %fusion.46 = f32[25,256,128]{2,1,0:T(8,128)} fusion(f32[25,257,130]{2,1,0:T(8,128)} %get-tuple-element.182, f32[25,257,130]{2,1,0:T(8,128)} %get-tuple-element.183, f32[25,256,128]{2,1,0:T(8,128)S(1)} %copy.160, f32[25,256,1]{2,1,0:T(8,128)} %copy.161, f32[25,256,1]{2,1,0:T(8,128)} %copy.159, f32[256,128]{1,0:T(8,128)} %copy.162, ...), kind=kLoop, calls=%fused_computation.13.clone.1 | loop fusion | flops 15564800 | bytes 26920960 | tf_op jit(solution)/shard_map/while/body/eval_jaxpr/add | solution.py:56
  591.2 4.7 collective-permute-start
  595.9 3.7 copy.160
  608.8 5.2 collective-permute-start.3
  620.7 14.4 %pad_maximum_fusion.15 = (f32[25,257,130]{2,1,0:T(8,128)}, f32[25,257,130]{2,1,0:T(8,128)}) fusion(f32[25,1,130]{2,1,0:T(1,128)} %collective-permute-done.2, f32[25,256,1]{2,1,0:T(8,128)} %copy.159, f32[25,256,128]{2,1,0:T(8,128)S(1)} %copy.160, f32[25,256,1]{2,1,0:T(8,128)} %copy.161, f32[25,1,130]{2,1,0:T(1,128)} %collective-permute-done.3), kind=kLoop, calls=%fused_computation.9.clone.1 | loop fusion | flops 5011500 | bytes 10036000 | tf_op jit(solution)/shard_map/while/body/eval_jaxpr/concatenate | solution.py:15
  635.1 17.5 %fusion.46 = f32[25,256,128]{2,1,0:T(8,128)} fusion(f32[25,257,130]{2,1,0:T(8,128)} %get-tuple-element.182, f32[25,257,130]{2,1,0:T(8,128)} %get-tuple-element.183, f32[25,256,128]{2,1,0:T(8,128)S(1)} %copy.160, f32[25,256,1]{2,1,0:T(8,128)} %copy.161, f32[25,256,1]{2,1,0:T(8,128)} %copy.159, f32[256,128]{1,0:T(8,128)} %copy.162, ...), kind=kLoop, calls=%fused_computation.13.clone.1 | loop fusion | flops 15564800 | bytes 26920960 | tf_op jit(solution)/shard_map/while/body/eval_jaxpr/add | solution.py:56
  657.9 4.7 collective-permute-start
  675.4 5.2 collective-permute-start.3
  687.3 14.4 %pad_maximum_fusion.15 = (f32[25,257,130]{2,1,0:T(8,128)}, f32[25,257,130]{2,1,0:T(8,128)}) fusion(f32[25,1,130]{2,1,0:T(1,128)} %collective-permute-done.2, f32[25,256,1]{2,1,0:T(8,128)} %copy.159, f32[25,256,128]{2,1,0:T(8,128)S(1)} %copy.160, f32[25,256,1]{2,1,0:T(8,128)} %copy.161, f32[25,1,130]{2,1,0:T(1,128)} %collective-permute-done.3), kind=kLoop, calls=%fused_computation.9.clone.1 | loop fusion | flops 5011500 | bytes 10036000 | tf_op jit(solution)/shard_map/while/body/eval_jaxpr/concatenate | solution.py:15
  701.7 17.5 %fusion.46 = f32[25,256,128]{2,1,0:T(8,128)} fusion(f32[25,257,130]{2,1,0:T(8,128)} %get-tuple-element.182, f32[25,257,130]{2,1,0:T(8,128)} %get-tuple-element.183, f32[25,256,128]{2,1,0:T(8,128)S(1)} %copy.160, f32[25,256,1]{2,1,0:T(8,128)} %copy.161, f32[25,256,1]{2,1,0:T(8,128)} %copy.159, f32[256,128]{1,0:T(8,128)} %copy.162, ...), kind=kLoop, calls=%fused_computation.13.clone.1 | loop fusion | flops 15564800 | bytes 26920960 | tf_op jit(solution)/shard_map/while/body/eval_jaxpr/add | solution.py:56
  724.5 4.7 collective-permute-start
  742.0 5.2 collective-permute-start.3
  753.9 14.4 %pad_maximum_fusion.15 = (f32[25,257,130]{2,1,0:T(8,128)}, f32[25,257,130]{2,1,0:T(8,128)}) fusion(f32[25,1,130]{2,1,0:T(1,128)} %collective-permute-done.2, f32[25,256,1]{2,1,0:T(8,128)} %copy.159, f32[25,256,128]{2,1,0:T(8,128)S(1)} %copy.160, f32[25,256,1]{2,1,0:T(8,128)} %copy.161, f32[25,1,130]{2,1,0:T(1,128)} %collective-permute-done.3), kind=kLoop, calls=%fused_computation.9.clone.1 | loop fusion | flops 5011500 | bytes 10036000 | tf_op jit(solution)/shard_map/while/body/eval_jaxpr/concatenate | solution.py:15
  768.3 17.5 %fusion.46 = f32[25,256,128]{2,1,0:T(8,128)} fusion(f32[25,257,130]{2,1,0:T(8,128)} %get-tuple-element.182, f32[25,257,130]{2,1,0:T(8,128)} %get-tuple-element.183, f32[25,256,128]{2,1,0:T(8,128)S(1)} %copy.160, f32[25,256,1]{2,1,0:T(8,128)} %copy.161, f32[25,256,1]{2,1,0:T(8,128)} %copy.159, f32[256,128]{1,0:T(8,128)} %copy.162, ...), kind=kLoop, calls=%fused_computation.13.clone.1 | loop fusion | flops 15564800 | bytes 26920960 | tf_op jit(solution)/shard_map/while/body/eval_jaxpr/add | solution.py:56
  791.1 4.7 collective-permute-start
  808.7 5.2 collective-permute-start.3
  820.6 14.4 %pad_maximum_fusion.15 = (f32[25,257,130]{2,1,0:T(8,128)}, f32[25,257,130]{2,1,0:T(8,128)}) fusion(f32[25,1,130]{2,1,0:T(1,128)} %collective-permute-done.2, f32[25,256,1]{2,1,0:T(8,128)} %copy.159, f32[25,256,128]{2,1,0:T(8,128)S(1)} %copy.160, f32[25,256,1]{2,1,0:T(8,128)} %copy.161, f32[25,1,130]{2,1,0:T(1,128)} %collective-permute-done.3), kind=kLoop, calls=%fused_computation.9.clone.1 | loop fusion | flops 5011500 | bytes 10036000 | tf_op jit(solution)/shard_map/while/body/eval_jaxpr/concatenate | solution.py:15
  835.0 17.5 %fusion.46 = f32[25,256,128]{2,1,0:T(8,128)} fusion(f32[25,257,130]{2,1,0:T(8,128)} %get-tuple-element.182, f32[25,257,130]{2,1,0:T(8,128)} %get-tuple-element.183, f32[25,256,128]{2,1,0:T(8,128)S(1)} %copy.160, f32[25,256,1]{2,1,0:T(8,128)} %copy.161, f32[25,256,1]{2,1,0:T(8,128)} %copy.159, f32[256,128]{1,0:T(8,128)} %copy.162, ...), kind=kLoop, calls=%fused_computation.13.clone.1 | loop fusion | flops 15564800 | bytes 26920960 | tf_op jit(solution)/shard_map/while/body/eval_jaxpr/add | solution.py:56
  862.4 9.0 copy.133
  871.5 8.6 gather_fusion.3
  880.1 8.6 gather_fusion.2
  888.7 8.6 gather_fusion.1
  897.3 8.6 gather_fusion
  906.9 19.4 %all_to_all.41 = f32[128,1,200]{2,1,0:T(1,128)S(1)} all-to-all(f32[128,1,200]{2,1,0:T(1,128)S(1)} %reshape.502), channel_id=1, replica_groups=mesh['lat'=8,'lon'=16] {'lat','lon'}, dimensions={0} | all-to-all | bytes 204800 | tf_op jit(solution)/shard_map/all_to_all | solution.py:143
  (433 shorter events, 282.7 us)
Async XLA Ops:
  3.3 30.7 %all-to-all-start.2 = ((s32[1,16,2]{2,0,1:T(1,128)}), s32[1,16,2]{2,0,1:T(1,128)}, u32[]{:S(2)}, u32[]{:S(2)}) async-start(s32[1,16,2]{2,0,1:T(1,128)} %bitcast.19), calls=%async_computation.2 | async-start | bytes 16384 | tf_op jit(solution)/shard_map/all_to_all | solution.py:86
  17.5 57.0 %collective-permute-start.4 = (f32[4,256,2]{1,2,0:T(2,128)}, f32[4,256,2]{1,2,0:T(2,128)S(1)}, u32[]{:S(2)}, u32[]{:S(2)}) collective-permute-start(f32[4,256,2]{1,2,0:T(2,128)} %get-tuple-element.95), channel_id=1, source_target_pairs={{0,1},{1,2},{2,3},{3,4},{4,5},{5,6},{6,7},{7,8},{8,9},{9,10},{10,1... | collective-permute-start | bytes 24584 | tf_op jit(solution)/shard_map/ppermute | solution.py:17
  19.2 55.4 %collective-permute-start.5 = (f32[4,256,2]{1,2,0:T(2,128)}, f32[4,256,2]{1,2,0:T(2,128)S(1)}, u32[]{:S(2)}, u32[]{:S(2)}) collective-permute-start(f32[4,256,2]{1,2,0:T(2,128)} %get-tuple-element.96), channel_id=1, source_target_pairs={{1,0},{2,1},{3,2},{4,3},{5,4},{6,5},{7,6},{8,7},{9,8},{10,9},{11,1... | collective-permute-start | bytes 24584 | tf_op jit(solution)/shard_map/ppermute | solution.py:19
  34.0 20.3 %all-to-all-start = ((s32[1,128,8]{2,0,1:T(1,128)}), s32[1,128,8]{2,0,1:T(1,128)S(1)}, u32[]{:S(2)}, u32[]{:S(2)}) async-start(s32[1,128,8]{2,0,1:T(1,128)} %bitcast.170), calls=%async_computation | async-start | bytes 131072 | tf_op jit(solution)/shard_map/all_to_all | solution.py:108
  54.3 14.4 %all-to-all-start.1 = ((f32[128,1,232]{2,1,0:T(1,128)}), f32[128,1,232]{2,1,0:T(1,128)S(1)}, u32[]{:S(2)}, u32[]{:S(2)}) async-start(f32[128,1,232]{2,1,0:T(1,128)} %reshape.500), calls=%async_computation.1 | async-start | bytes 262144 | tf_op jit(solution)/shard_map/all_to_all | solution.py:107
  68.7 111.1 %all-to-all-start.3 = ((f32[25,32,8,128]{3,2,0,1:T(8,128)}), f32[25,32,8,128]{3,2,0,1:T(8,128)}, u32[]{:S(2)}, u32[]{:S(2)}) async-start(f32[25,32,8,128]{3,2,0,1:T(8,128)} %copy.123), calls=%async_computation.3 | async-start | bytes 6553600 | tf_op jit(solution)/shard_map/all_to_all | solution.py:85
  74.8 48.7 %collective-permute-start.6 = (f32[4,2,132]{1,2,0:T(8,128)S(1)}, f32[4,2,132]{1,2,0:T(8,128)S(1)}, u32[]{:S(2)}, u32[]{:S(2)}) collective-permute-start(f32[4,2,132]{1,2,0:T(8,128)S(1)} %get-tuple-element.89), channel_id=1, source_target_pairs={{0,16},{16,32},{32,48},{48,64},{64,80},{80,96},{96,112},{1,17},{17... | collective-permute-start | bytes 12680 | tf_op jit(solution)/shard_map/ppermute | solution.py:17
  77.1 46.4 %collective-permute-start.7 = (f32[4,2,132]{1,2,0:T(8,128)S(1)}, f32[4,2,132]{1,2,0:T(8,128)S(1)}, u32[]{:S(2)}, u32[]{:S(2)}) collective-permute-start(f32[4,2,132]{1,2,0:T(8,128)S(1)} %get-tuple-element.90), channel_id=1, source_target_pairs={{16,0},{32,16},{48,32},{64,48},{80,64},{96,80},{112,96},{17,1},{33... | collective-permute-start | bytes 12680 | tf_op jit(solution)/shard_map/ppermute | solution.py:19
  193.5 25.1 %copy-start.3 = (f32[1,256,128]{1,2,0:T(8,128)}, f32[1,256,128]{1,2,0:T(8,128)S(1)}, u32[]{:S(2)}) copy-start(f32[1,256,128]{1,2,0:T(8,128)S(1)} %get-tuple-element.206) | copy-start | bytes 393220 | tf_op jit(solution)/shard_map/while
  194.3 9.8 %collective-permute-start.1 = (f32[25,256,1]{1,2,0:T(1,128)}, f32[25,256,1]{1,2,0:T(1,128)}, u32[]{:S(2)}, u32[]{:S(2)}) collective-permute-start(f32[25,256,1]{1,2,0:T(1,128)} %get-tuple-element.179), channel_id=1, source_target_pairs={{0,1},{1,2},{2,3},{3,4},{4,5},{5,6},{6,7},{7,8},{8,9},{9,10},{10,1... | collective-permute-start | bytes 76808 | tf_op jit(solution)/shard_map/while/body/eval_jaxpr/ppermute | solution.py:17
  200.4 6.7 collective-permute-start
  211.9 13.3 %collective-permute-start.2 = (f32[25,1,130]{2,1,0:T(1,128)}, f32[25,1,130]{2,1,0:T(1,128)}, u32[]{:S(2)}, u32[]{:S(2)}) collective-permute-start(f32[25,1,130]{2,1,0:T(1,128)} %get-tuple-element.180), channel_id=1, source_target_pairs={{16,0},{32,16},{48,32},{64,48},{80,64},{96,80},{112,96},{17,1},{33... | collective-permute-start | bytes 39008 | tf_op jit(solution)/shard_map/while/body/eval_jaxpr/ppermute | solution.py:19
  213.2 12.1 %collective-permute-start.3 = (f32[25,1,130]{2,1,0:T(1,128)}, f32[25,1,130]{2,1,0:T(1,128)}, u32[]{:S(2)}, u32[]{:S(2)}) collective-permute-start(f32[25,1,130]{2,1,0:T(1,128)} %get-tuple-element.181), channel_id=1, source_target_pairs={{0,16},{16,32},{32,48},{48,64},{64,80},{80,96},{96,112},{1,17},{17... | collective-permute-start | bytes 39008 | tf_op jit(solution)/shard_map/while/body/eval_jaxpr/ppermute | solution.py:17
  261.6 5.7 collective-permute-start.1
  263.6 6.7 collective-permute-start
  275.1 13.2 %collective-permute-start.2 = (f32[25,1,130]{2,1,0:T(1,128)}, f32[25,1,130]{2,1,0:T(1,128)}, u32[]{:S(2)}, u32[]{:S(2)}) collective-permute-start(f32[25,1,130]{2,1,0:T(1,128)} %get-tuple-element.180), channel_id=1, source_target_pairs={{16,0},{32,16},{48,32},{64,48},{80,64},{96,80},{112,96},{17,1},{33... | collective-permute-start | bytes 39008 | tf_op jit(solution)/shard_map/while/body/eval_jaxpr/ppermute | solution.py:19
  276.4 11.9 %collective-permute-start.3 = (f32[25,1,130]{2,1,0:T(1,128)}, f32[25,1,130]{2,1,0:T(1,128)}, u32[]{:S(2)}, u32[]{:S(2)}) collective-permute-start(f32[25,1,130]{2,1,0:T(1,128)} %get-tuple-element.181), channel_id=1, source_target_pairs={{0,16},{16,32},{32,48},{48,64},{64,80},{80,96},{96,112},{1,17},{17... | collective-permute-start | bytes 39008 | tf_op jit(solution)/shard_map/while/body/eval_jaxpr/ppermute | solution.py:17
  323.8 23.5 %copy-start.3 = (f32[1,256,128]{1,2,0:T(8,128)}, f32[1,256,128]{1,2,0:T(8,128)S(1)}, u32[]{:S(2)}) copy-start(f32[1,256,128]{1,2,0:T(8,128)S(1)} %get-tuple-element.206) | copy-start | bytes 393220 | tf_op jit(solution)/shard_map/while
  324.6 8.4 collective-permute-start.1
  326.6 9.4 %collective-permute-start = (f32[25,256,1]{1,2,0:T(1,128)}, f32[25,256,1]{1,2,0:T(1,128)}, u32[]{:S(2)}, u32[]{:S(2)}) collective-permute-start(f32[25,256,1]{1,2,0:T(1,128)} %get-tuple-element.178), channel_id=1, source_target_pairs={{1,0},{2,1},{3,2},{4,3},{5,4},{6,5},{7,6},{8,7},{9,8},{10,9},{11,1... | collective-permute-start | bytes 76808 | tf_op jit(solution)/shard_map/while/body/eval_jaxpr/ppermute | solution.py:19
  340.9 13.2 %collective-permute-start.2 = (f32[25,1,130]{2,1,0:T(1,128)}, f32[25,1,130]{2,1,0:T(1,128)}, u32[]{:S(2)}, u32[]{:S(2)}) collective-permute-start(f32[25,1,130]{2,1,0:T(1,128)} %get-tuple-element.180), channel_id=1, source_target_pairs={{16,0},{32,16},{48,32},{64,48},{80,64},{96,80},{112,96},{17,1},{33... | collective-permute-start | bytes 39008 | tf_op jit(solution)/shard_map/while/body/eval_jaxpr/ppermute | solution.py:19
  342.2 11.9 %collective-permute-start.3 = (f32[25,1,130]{2,1,0:T(1,128)}, f32[25,1,130]{2,1,0:T(1,128)}, u32[]{:S(2)}, u32[]{:S(2)}) collective-permute-start(f32[25,1,130]{2,1,0:T(1,128)} %get-tuple-element.181), channel_id=1, source_target_pairs={{0,16},{16,32},{32,48},{48,64},{64,80},{80,96},{96,112},{1,17},{17... | collective-permute-start | bytes 39008 | tf_op jit(solution)/shard_map/while/body/eval_jaxpr/ppermute | solution.py:17
  389.6 24.4 %copy-start.3 = (f32[1,256,128]{1,2,0:T(8,128)}, f32[1,256,128]{1,2,0:T(8,128)S(1)}, u32[]{:S(2)}) copy-start(f32[1,256,128]{1,2,0:T(8,128)S(1)} %get-tuple-element.206) | copy-start | bytes 393220 | tf_op jit(solution)/shard_map/while
  390.4 9.3 %collective-permute-start.1 = (f32[25,256,1]{1,2,0:T(1,128)}, f32[25,256,1]{1,2,0:T(1,128)}, u32[]{:S(2)}, u32[]{:S(2)}) collective-permute-start(f32[25,256,1]{1,2,0:T(1,128)} %get-tuple-element.179), channel_id=1, source_target_pairs={{0,1},{1,2},{2,3},{3,4},{4,5},{5,6},{6,7},{7,8},{8,9},{9,10},{10,1... | collective-permute-start | bytes 76808 | tf_op jit(solution)/shard_map/while/body/eval_jaxpr/ppermute | solution.py:17
  391.3 11.4 %collective-permute-start = (f32[25,256,1]{1,2,0:T(1,128)}, f32[25,256,1]{1,2,0:T(1,128)}, u32[]{:S(2)}, u32[]{:S(2)}) collective-permute-start(f32[25,256,1]{1,2,0:T(1,128)} %get-tuple-element.178), channel_id=1, source_target_pairs={{1,0},{2,1},{3,2},{4,3},{5,4},{6,5},{7,6},{8,7},{9,8},{10,9},{11,1... | collective-permute-start | bytes 76808 | tf_op jit(solution)/shard_map/while/body/eval_jaxpr/ppermute | solution.py:19
  407.5 13.2 %collective-permute-start.2 = (f32[25,1,130]{2,1,0:T(1,128)}, f32[25,1,130]{2,1,0:T(1,128)}, u32[]{:S(2)}, u32[]{:S(2)}) collective-permute-start(f32[25,1,130]{2,1,0:T(1,128)} %get-tuple-element.180), channel_id=1, source_target_pairs={{16,0},{32,16},{48,32},{64,48},{80,64},{96,80},{112,96},{17,1},{33... | collective-permute-start | bytes 39008 | tf_op jit(solution)/shard_map/while/body/eval_jaxpr/ppermute | solution.py:19
  408.8 11.9 %collective-permute-start.3 = (f32[25,1,130]{2,1,0:T(1,128)}, f32[25,1,130]{2,1,0:T(1,128)}, u32[]{:S(2)}, u32[]{:S(2)}) collective-permute-start(f32[25,1,130]{2,1,0:T(1,128)} %get-tuple-element.181), channel_id=1, source_target_pairs={{0,16},{16,32},{32,48},{48,64},{64,80},{80,96},{96,112},{1,17},{17... | collective-permute-start | bytes 39008 | tf_op jit(solution)/shard_map/while/body/eval_jaxpr/ppermute | solution.py:17
  456.2 24.4 %copy-start.3 = (f32[1,256,128]{1,2,0:T(8,128)}, f32[1,256,128]{1,2,0:T(8,128)S(1)}, u32[]{:S(2)}) copy-start(f32[1,256,128]{1,2,0:T(8,128)S(1)} %get-tuple-element.206) | copy-start | bytes 393220 | tf_op jit(solution)/shard_map/while
  457.0 9.3 %collective-permute-start.1 = (f32[25,256,1]{1,2,0:T(1,128)}, f32[25,256,1]{1,2,0:T(1,128)}, u32[]{:S(2)}, u32[]{:S(2)}) collective-permute-start(f32[25,256,1]{1,2,0:T(1,128)} %get-tuple-element.179), channel_id=1, source_target_pairs={{0,1},{1,2},{2,3},{3,4},{4,5},{5,6},{6,7},{7,8},{8,9},{9,10},{10,1... | collective-permute-start | bytes 76808 | tf_op jit(solution)/shard_map/while/body/eval_jaxpr/ppermute | solution.py:17
  457.9 11.4 %collective-permute-start = (f32[25,256,1]{1,2,0:T(1,128)}, f32[25,256,1]{1,2,0:T(1,128)}, u32[]{:S(2)}, u32[]{:S(2)}) collective-permute-start(f32[25,256,1]{1,2,0:T(1,128)} %get-tuple-element.178), channel_id=1, source_target_pairs={{1,0},{2,1},{3,2},{4,3},{5,4},{6,5},{7,6},{8,7},{9,8},{10,9},{11,1... | collective-permute-start | bytes 76808 | tf_op jit(solution)/shard_map/while/body/eval_jaxpr/ppermute | solution.py:19
  474.2 13.2 %collective-permute-start.2 = (f32[25,1,130]{2,1,0:T(1,128)}, f32[25,1,130]{2,1,0:T(1,128)}, u32[]{:S(2)}, u32[]{:S(2)}) collective-permute-start(f32[25,1,130]{2,1,0:T(1,128)} %get-tuple-element.180), channel_id=1, source_target_pairs={{16,0},{32,16},{48,32},{64,48},{80,64},{96,80},{112,96},{17,1},{33... | collective-permute-start | bytes 39008 | tf_op jit(solution)/shard_map/while/body/eval_jaxpr/ppermute | solution.py:19
  475.5 11.9 %collective-permute-start.3 = (f32[25,1,130]{2,1,0:T(1,128)}, f32[25,1,130]{2,1,0:T(1,128)}, u32[]{:S(2)}, u32[]{:S(2)}) collective-permute-start(f32[25,1,130]{2,1,0:T(1,128)} %get-tuple-element.181), channel_id=1, source_target_pairs={{0,16},{16,32},{32,48},{48,64},{64,80},{80,96},{96,112},{1,17},{17... | collective-permute-start | bytes 39008 | tf_op jit(solution)/shard_map/while/body/eval_jaxpr/ppermute | solution.py:17
  522.9 24.4 %copy-start.3 = (f32[1,256,128]{1,2,0:T(8,128)}, f32[1,256,128]{1,2,0:T(8,128)S(1)}, u32[]{:S(2)}) copy-start(f32[1,256,128]{1,2,0:T(8,128)S(1)} %get-tuple-element.206) | copy-start | bytes 393220 | tf_op jit(solution)/shard_map/while
  523.6 9.3 %collective-permute-start.1 = (f32[25,256,1]{1,2,0:T(1,128)}, f32[25,256,1]{1,2,0:T(1,128)}, u32[]{:S(2)}, u32[]{:S(2)}) collective-permute-start(f32[25,256,1]{1,2,0:T(1,128)} %get-tuple-element.179), channel_id=1, source_target_pairs={{0,1},{1,2},{2,3},{3,4},{4,5},{5,6},{6,7},{7,8},{8,9},{9,10},{10,1... | collective-permute-start | bytes 76808 | tf_op jit(solution)/shard_map/while/body/eval_jaxpr/ppermute | solution.py:17
  524.6 11.4 %collective-permute-start = (f32[25,256,1]{1,2,0:T(1,128)}, f32[25,256,1]{1,2,0:T(1,128)}, u32[]{:S(2)}, u32[]{:S(2)}) collective-permute-start(f32[25,256,1]{1,2,0:T(1,128)} %get-tuple-element.178), channel_id=1, source_target_pairs={{1,0},{2,1},{3,2},{4,3},{5,4},{6,5},{7,6},{8,7},{9,8},{10,9},{11,1... | collective-permute-start | bytes 76808 | tf_op jit(solution)/shard_map/while/body/eval_jaxpr/ppermute | solution.py:19
  540.8 13.2 %collective-permute-start.2 = (f32[25,1,130]{2,1,0:T(1,128)}, f32[25,1,130]{2,1,0:T(1,128)}, u32[]{:S(2)}, u32[]{:S(2)}) collective-permute-start(f32[25,1,130]{2,1,0:T(1,128)} %get-tuple-element.180), channel_id=1, source_target_pairs={{16,0},{32,16},{48,32},{64,48},{80,64},{96,80},{112,96},{17,1},{33... | collective-permute-start | bytes 39008 | tf_op jit(solution)/shard_map/while/body/eval_jaxpr/ppermute | solution.py:19
  542.1 11.9 %collective-permute-start.3 = (f32[25,1,130]{2,1,0:T(1,128)}, f32[25,1,130]{2,1,0:T(1,128)}, u32[]{:S(2)}, u32[]{:S(2)}) collective-permute-start(f32[25,1,130]{2,1,0:T(1,128)} %get-tuple-element.181), channel_id=1, source_target_pairs={{0,16},{16,32},{32,48},{48,64},{64,80},{80,96},{96,112},{1,17},{17... | collective-permute-start | bytes 39008 | tf_op jit(solution)/shard_map/while/body/eval_jaxpr/ppermute | solution.py:17
  589.5 24.4 %copy-start.3 = (f32[1,256,128]{1,2,0:T(8,128)}, f32[1,256,128]{1,2,0:T(8,128)S(1)}, u32[]{:S(2)}) copy-start(f32[1,256,128]{1,2,0:T(8,128)S(1)} %get-tuple-element.206) | copy-start | bytes 393220 | tf_op jit(solution)/shard_map/while
  590.3 9.3 %collective-permute-start.1 = (f32[25,256,1]{1,2,0:T(1,128)}, f32[25,256,1]{1,2,0:T(1,128)}, u32[]{:S(2)}, u32[]{:S(2)}) collective-permute-start(f32[25,256,1]{1,2,0:T(1,128)} %get-tuple-element.179), channel_id=1, source_target_pairs={{0,1},{1,2},{2,3},{3,4},{4,5},{5,6},{6,7},{7,8},{8,9},{9,10},{10,1... | collective-permute-start | bytes 76808 | tf_op jit(solution)/shard_map/while/body/eval_jaxpr/ppermute | solution.py:17
  591.2 11.4 %collective-permute-start = (f32[25,256,1]{1,2,0:T(1,128)}, f32[25,256,1]{1,2,0:T(1,128)}, u32[]{:S(2)}, u32[]{:S(2)}) collective-permute-start(f32[25,256,1]{1,2,0:T(1,128)} %get-tuple-element.178), channel_id=1, source_target_pairs={{1,0},{2,1},{3,2},{4,3},{5,4},{6,5},{7,6},{8,7},{9,8},{10,9},{11,1... | collective-permute-start | bytes 76808 | tf_op jit(solution)/shard_map/while/body/eval_jaxpr/ppermute | solution.py:19
  607.5 13.2 %collective-permute-start.2 = (f32[25,1,130]{2,1,0:T(1,128)}, f32[25,1,130]{2,1,0:T(1,128)}, u32[]{:S(2)}, u32[]{:S(2)}) collective-permute-start(f32[25,1,130]{2,1,0:T(1,128)} %get-tuple-element.180), channel_id=1, source_target_pairs={{16,0},{32,16},{48,32},{64,48},{80,64},{96,80},{112,96},{17,1},{33... | collective-permute-start | bytes 39008 | tf_op jit(solution)/shard_map/while/body/eval_jaxpr/ppermute | solution.py:19
  608.8 11.9 %collective-permute-start.3 = (f32[25,1,130]{2,1,0:T(1,128)}, f32[25,1,130]{2,1,0:T(1,128)}, u32[]{:S(2)}, u32[]{:S(2)}) collective-permute-start(f32[25,1,130]{2,1,0:T(1,128)} %get-tuple-element.181), channel_id=1, source_target_pairs={{0,16},{16,32},{32,48},{48,64},{64,80},{80,96},{96,112},{1,17},{17... | collective-permute-start | bytes 39008 | tf_op jit(solution)/shard_map/while/body/eval_jaxpr/ppermute | solution.py:17
  656.2 24.4 %copy-start.3 = (f32[1,256,128]{1,2,0:T(8,128)}, f32[1,256,128]{1,2,0:T(8,128)S(1)}, u32[]{:S(2)}) copy-start(f32[1,256,128]{1,2,0:T(8,128)S(1)} %get-tuple-element.206) | copy-start | bytes 393220 | tf_op jit(solution)/shard_map/while
  656.9 9.3 %collective-permute-start.1 = (f32[25,256,1]{1,2,0:T(1,128)}, f32[25,256,1]{1,2,0:T(1,128)}, u32[]{:S(2)}, u32[]{:S(2)}) collective-permute-start(f32[25,256,1]{1,2,0:T(1,128)} %get-tuple-element.179), channel_id=1, source_target_pairs={{0,1},{1,2},{2,3},{3,4},{4,5},{5,6},{6,7},{7,8},{8,9},{9,10},{10,1... | collective-permute-start | bytes 76808 | tf_op jit(solution)/shard_map/while/body/eval_jaxpr/ppermute | solution.py:17
  657.9 11.4 %collective-permute-start = (f32[25,256,1]{1,2,0:T(1,128)}, f32[25,256,1]{1,2,0:T(1,128)}, u32[]{:S(2)}, u32[]{:S(2)}) collective-permute-start(f32[25,256,1]{1,2,0:T(1,128)} %get-tuple-element.178), channel_id=1, source_target_pairs={{1,0},{2,1},{3,2},{4,3},{5,4},{6,5},{7,6},{8,7},{9,8},{10,9},{11,1... | collective-permute-start | bytes 76808 | tf_op jit(solution)/shard_map/while/body/eval_jaxpr/ppermute | solution.py:19
  674.1 13.2 %collective-permute-start.2 = (f32[25,1,130]{2,1,0:T(1,128)}, f32[25,1,130]{2,1,0:T(1,128)}, u32[]{:S(2)}, u32[]{:S(2)}) collective-permute-start(f32[25,1,130]{2,1,0:T(1,128)} %get-tuple-element.180), channel_id=1, source_target_pairs={{16,0},{32,16},{48,32},{64,48},{80,64},{96,80},{112,96},{17,1},{33... | collective-permute-start | bytes 39008 | tf_op jit(solution)/shard_map/while/body/eval_jaxpr/ppermute | solution.py:19
  675.4 11.9 %collective-permute-start.3 = (f32[25,1,130]{2,1,0:T(1,128)}, f32[25,1,130]{2,1,0:T(1,128)}, u32[]{:S(2)}, u32[]{:S(2)}) collective-permute-start(f32[25,1,130]{2,1,0:T(1,128)} %get-tuple-element.181), channel_id=1, source_target_pairs={{0,16},{16,32},{32,48},{48,64},{64,80},{80,96},{96,112},{1,17},{17... | collective-permute-start | bytes 39008 | tf_op jit(solution)/shard_map/while/body/eval_jaxpr/ppermute | solution.py:17
  722.8 24.4 %copy-start.3 = (f32[1,256,128]{1,2,0:T(8,128)}, f32[1,256,128]{1,2,0:T(8,128)S(1)}, u32[]{:S(2)}) copy-start(f32[1,256,128]{1,2,0:T(8,128)S(1)} %get-tuple-element.206) | copy-start | bytes 393220 | tf_op jit(solution)/shard_map/while
  723.6 9.3 %collective-permute-start.1 = (f32[25,256,1]{1,2,0:T(1,128)}, f32[25,256,1]{1,2,0:T(1,128)}, u32[]{:S(2)}, u32[]{:S(2)}) collective-permute-start(f32[25,256,1]{1,2,0:T(1,128)} %get-tuple-element.179), channel_id=1, source_target_pairs={{0,1},{1,2},{2,3},{3,4},{4,5},{5,6},{6,7},{7,8},{8,9},{9,10},{10,1... | collective-permute-start | bytes 76808 | tf_op jit(solution)/shard_map/while/body/eval_jaxpr/ppermute | solution.py:17
  724.5 11.4 %collective-permute-start = (f32[25,256,1]{1,2,0:T(1,128)}, f32[25,256,1]{1,2,0:T(1,128)}, u32[]{:S(2)}, u32[]{:S(2)}) collective-permute-start(f32[25,256,1]{1,2,0:T(1,128)} %get-tuple-element.178), channel_id=1, source_target_pairs={{1,0},{2,1},{3,2},{4,3},{5,4},{6,5},{7,6},{8,7},{9,8},{10,9},{11,1... | collective-permute-start | bytes 76808 | tf_op jit(solution)/shard_map/while/body/eval_jaxpr/ppermute | solution.py:19
  740.7 13.2 %collective-permute-start.2 = (f32[25,1,130]{2,1,0:T(1,128)}, f32[25,1,130]{2,1,0:T(1,128)}, u32[]{:S(2)}, u32[]{:S(2)}) collective-permute-start(f32[25,1,130]{2,1,0:T(1,128)} %get-tuple-element.180), channel_id=1, source_target_pairs={{16,0},{32,16},{48,32},{64,48},{80,64},{96,80},{112,96},{17,1},{33... | collective-permute-start | bytes 39008 | tf_op jit(solution)/shard_map/while/body/eval_jaxpr/ppermute | solution.py:19
  742.0 11.9 %collective-permute-start.3 = (f32[25,1,130]{2,1,0:T(1,128)}, f32[25,1,130]{2,1,0:T(1,128)}, u32[]{:S(2)}, u32[]{:S(2)}) collective-permute-start(f32[25,1,130]{2,1,0:T(1,128)} %get-tuple-element.181), channel_id=1, source_target_pairs={{0,16},{16,32},{32,48},{48,64},{64,80},{80,96},{96,112},{1,17},{17... | collective-permute-start | bytes 39008 | tf_op jit(solution)/shard_map/while/body/eval_jaxpr/ppermute | solution.py:17
  789.4 24.4 %copy-start.3 = (f32[1,256,128]{1,2,0:T(8,128)}, f32[1,256,128]{1,2,0:T(8,128)S(1)}, u32[]{:S(2)}) copy-start(f32[1,256,128]{1,2,0:T(8,128)S(1)} %get-tuple-element.206) | copy-start | bytes 393220 | tf_op jit(solution)/shard_map/while
  790.2 9.3 %collective-permute-start.1 = (f32[25,256,1]{1,2,0:T(1,128)}, f32[25,256,1]{1,2,0:T(1,128)}, u32[]{:S(2)}, u32[]{:S(2)}) collective-permute-start(f32[25,256,1]{1,2,0:T(1,128)} %get-tuple-element.179), channel_id=1, source_target_pairs={{0,1},{1,2},{2,3},{3,4},{4,5},{5,6},{6,7},{7,8},{8,9},{9,10},{10,1... | collective-permute-start | bytes 76808 | tf_op jit(solution)/shard_map/while/body/eval_jaxpr/ppermute | solution.py:17
  791.1 11.4 %collective-permute-start = (f32[25,256,1]{1,2,0:T(1,128)}, f32[25,256,1]{1,2,0:T(1,128)}, u32[]{:S(2)}, u32[]{:S(2)}) collective-permute-start(f32[25,256,1]{1,2,0:T(1,128)} %get-tuple-element.178), channel_id=1, source_target_pairs={{1,0},{2,1},{3,2},{4,3},{5,4},{6,5},{7,6},{8,7},{9,8},{10,9},{11,1... | collective-permute-start | bytes 76808 | tf_op jit(solution)/shard_map/while/body/eval_jaxpr/ppermute | solution.py:19
  807.4 13.2 %collective-permute-start.2 = (f32[25,1,130]{2,1,0:T(1,128)}, f32[25,1,130]{2,1,0:T(1,128)}, u32[]{:S(2)}, u32[]{:S(2)}) collective-permute-start(f32[25,1,130]{2,1,0:T(1,128)} %get-tuple-element.180), channel_id=1, source_target_pairs={{16,0},{32,16},{48,32},{64,48},{80,64},{96,80},{112,96},{17,1},{33... | collective-permute-start | bytes 39008 | tf_op jit(solution)/shard_map/while/body/eval_jaxpr/ppermute | solution.py:19
  808.7 11.9 %collective-permute-start.3 = (f32[25,1,130]{2,1,0:T(1,128)}, f32[25,1,130]{2,1,0:T(1,128)}, u32[]{:S(2)}, u32[]{:S(2)}) collective-permute-start(f32[25,1,130]{2,1,0:T(1,128)} %get-tuple-element.181), channel_id=1, source_target_pairs={{0,16},{16,32},{32,48},{48,64},{64,80},{80,96},{96,112},{1,17},{17... | collective-permute-start | bytes 39008 | tf_op jit(solution)/shard_map/while/body/eval_jaxpr/ppermute | solution.py:17
  862.4 26.3 %copy-start.20 = (s32[1024]{0:T(1024)S(1)}, s32[1024]{0:T(1024)}, u32[]{:S(2)}) copy-start(s32[1024]{0:T(1024)} %get-tuple-element.128) | copy-start | bytes 12292
  871.4 25.9 %copy-start.19 = (s32[1024]{0:T(1024)S(1)}, s32[1024]{0:T(1024)}, u32[]{:S(2)}) copy-start(s32[1024]{0:T(1024)} %broadcast_clamp_fusion.3) | copy-start | bytes 12292
  871.4 34.5 %copy-start.12 = (f32[1,128,8]{2,1,0:T(8,128)S(1)}, f32[1,128,8]{2,1,0:T(8,128)}, u32[]{:S(2)}) copy-start(f32[1,128,8]{2,1,0:T(8,128)} %copy.146) | copy-start | bytes 12292
  871.4 34.5 %copy-start.13 = (f32[1,128,8]{2,1,0:T(8,128)S(1)}, f32[1,128,8]{2,1,0:T(8,128)}, u32[]{:S(2)}) copy-start(f32[1,128,8]{2,1,0:T(8,128)} %copy.147) | copy-start | bytes 12292
  871.4 34.5 %copy-start.14 = (f32[1,128,8]{2,1,0:T(8,128)S(1)}, f32[1,128,8]{2,1,0:T(8,128)}, u32[]{:S(2)}) copy-start(f32[1,128,8]{2,1,0:T(8,128)} %copy.148) | copy-start | bytes 12292
  871.5 34.5 %copy-start.15 = (f32[1,128,8]{2,1,0:T(8,128)S(1)}, f32[1,128,8]{2,1,0:T(8,128)}, u32[]{:S(2)}) copy-start(f32[1,128,8]{2,1,0:T(8,128)} %copy.149) | copy-start | bytes 12292
  897.3 30.3 %copy-start.22 = (s32[1024]{0:T(1024)S(1)}, s32[1024]{0:T(1024)}, u32[]{:S(2)}) copy-start(s32[1024]{0:T(1024)} %get-tuple-element.125) | copy-start | bytes 12292
  (67 other events, 513.3 us)
where the time goes:
time: 934 us; the launch traced here: 929 us
  other arithmetic  394 us (42%)
  local copies, waits for them, and re-layouts  308 us (33%)
  starting transfers between devices  145 us (16%)
  waiting for transfers between devices  60.4 us (6%)
  blocking collectives  19.4 us (2%)
    add x10, other arithmetic, advance(): centre + east_face * (padded[:, 1:-1, 2:] - centre)  175 us
    concatenate x12, other arithmetic, with_halo(): jnp.concatenate([lax.ppermute(tail, axis, [(i, (i + 1) % count) for i in...  144 us
    another operation x23, local copies, waits for them, and re-layouts  72.4 us
    ppermute x22, starting transfers between devices, with_halo(): lax.ppermute(tail, axis, [(i, (i + 1) % count) for i in range(ends)])  66.1 us
    ppermute x22, starting transfers between devices, with_halo(): lax.ppermute(head, axis, [((i + 1) % count, i) for i in range(ends)])  49.9 us
    ppermute x22, waiting for transfers between devices, with_halo(): lax.ppermute(tail, axis, [(i, (i + 1) % count) for i in range(ends)])  44.4 us
    ppermute x10, local copies, waits for them, and re-layouts, with_halo(): lax.ppermute(tail, axis, [(i, (i + 1) % count) for i in range(ends)])  29.6 us
    ppermute x10, local copies, waits for them, and re-layouts, with_halo(): lax.ppermute(head, axis, [((i + 1) % count, i) for i in range(ends)])  29.4 us
  transfers between devices with their start and end apart: 48, of which 3 were waited for; matrix products, arithmetic and copies ran while one was open for 23% of the time, Pallas kernels for 0%

commit v1 on v0

--- a/solution.py
+++ b/solution.py
@@ -140,7 +140,13 @@
         + recv_weights[2][None, :] * flat_field[:, base_cell + lon_cells]
         + recv_weights[3][None, :] * flat_field[:, base_cell + lon_cells + 1]
     )
-    returned = lax.all_to_all(sampled, ("lat", "lon"), split_axis=1, concat_axis=1, tiled=True)
+    fill_the_pipes = lambda target, shard_axis: jnp.concatenate(
+        lax.all_to_all(
+            jnp.stack(jnp.split(target, lax.axis_size(shard_axis), 1), 0), shard_axis, 0, 0
+        ),
+        axis=1,
+    )
+    returned = fill_the_pipes(sampled, ("lat", "lon"))
     profile_values = returned[:, slot_of]
     return (smoothed, profile_values)
 

time: 934 us -> 896 us (0.959)
  local copies, waits for them, and re-layouts: 308 us -> 280 us
    mul x10, local copies, waits for them, and re-layouts: 0.87 us -> 16.5 us  [advance(): east_face * (padded[:, 1:-1, 2:] - centre)]
    mul x10, local copies, waits for them, and re-layouts: 16.5 us -> 0.88 us  [advance(): 0.25 * twist_face]
    another operation x23 -> x24, local copies, waits for them, and re-layouts: 72.4 us -> 72.4 us
  transfers between devices with their start and end apart: 48 -> 48, of which waited for: 3 -> 3; matrix products, arithmetic and copies ran while one was open for 23% -> 22% of each run, Pallas kernels for 0% -> 0%
where the time goes in v1:
time: 896 us; the launch traced here: 892 us
  other arithmetic  387 us (43%)
  local copies, waits for them, and re-layouts  280 us (31%)
  starting transfers between devices  139 us (16%)
  waiting for transfers between devices  60.6 us (7%)
  blocking collectives  21.8 us (2%)
    add x10, other arithmetic, advance(): centre + east_face * (padded[:, 1:-1, 2:] - centre)  175 us
    concatenate x12, other arithmetic, with_halo(): jnp.concatenate([lax.ppermute(tail, axis, [(i, (i + 1) % count) for i in...  144 us
    another operation x23, local copies, waits for them, and re-layouts  72.4 us
    ppermute x22, starting transfers between devices, with_halo(): lax.ppermute(tail, axis, [(i, (i + 1) % count) for i in range(ends)])  60.1 us
    ppermute x22, starting transfers between devices, with_halo(): lax.ppermute(head, axis, [((i + 1) % count, i) for i in range(ends)])  52.6 us
    ppermute x22, waiting for transfers between devices, with_halo(): lax.ppermute(tail, axis, [(i, (i + 1) % count) for i in range(ends)])  44.4 us
    scatter-add x1, other arithmetic, on_device(): jnp.zeros((levels, lat_cells * lon_cells), jnp.float32).at[:, corner_cells]  29.1 us
    ppermute x10, local copies, waits for them, and re-layouts, with_halo(): lax.ppermute(tail, axis, [(i, (i + 1) % count) for i in range(ends)])  23.4 us
  transfers between devices with their start and end apart: 48, of which 3 were waited for; matrix products, arithmetic and copies ran while one was open for 22% of the time, Pallas kernels for 0%

profile of v1, /device:TPU:1, one launch (start us, length us, event | category | flops | bytes accessed | tf_op | source)
XLA Modules:
  0.0 892.5 jit_solution(15531985250861903136)
XLA Ops:
  10.9 8.3 all-to-all-start.2
  27.0 4.0 copy.555
  34.1 9.3 %all-to-all-start = ((s32[1,128,8]{2,0,1:T(1,128)}), s32[1,128,8]{2,0,1:T(1,128)S(1)}, u32[]{:S(2)}, u32[]{:S(2)}) async-start(s32[1,128,8]{2,0,1:T(1,128)} %bitcast.635), calls=%async_computation | async-start | bytes 131072 | tf_op jit(solution)/shard_map/all_to_all | solution.py:108
  45.4 7.8 all-to-all-done
  53.2 4.3 all-to-all-start.1
  59.2 8.4 all-to-all-done.1
  67.6 4.6 all-to-all-start.3
  78.0 44.3 %collective-permute-done.6 = f32[4,2,132]{1,2,0:T(8,128)S(1)} collective-permute-done((f32[4,2,132]{1,2,0:T(8,128)S(1)}, f32[4,2,132]{1,2,0:T(8,128)S(1)}, u32[]{:S(2)}, u32[]{:S(2)}) %collective-permute-start.6) | collective-permute-done | bytes 4256 | tf_op jit(solution)/shard_map/ppermute | solution.py:17
  130.0 29.1 %scatter_custom_fusion.2 = f32[25,32768]{0,1:T(8,128)} fusion(s32[4096]{0:T(1024)S(1)} %bitcast.639, f32[4096,25]{1,0:T(8,128)S(1)} %copy.553, f32[]{:T(128)} %constant.8.clone.1), kind=kCustom, calls=%fused_computation.34 | custom fusion | flops 102400 | bytes 3276804 | tf_op jit(solution)/shard_map/scatter-add | solution.py:120
  159.2 13.8 %copy.556 = f32[25,256,128]{1,2,0:T(8,128)} copy(f32[25,256,128]{0,2,1:T(8,128)} %bitcast.610) | data formatting | bytes 6553600 | tf_op jit(solution)/shard_map/reshape | solution.py:122
  173.6 5.0 scatter_fusion
  181.8 4.6 add_multiply_fusion
  186.4 628.8 %while.10 = (s32[]{:T(128)}, f32[25,256,128]{1,2,0:T(8,128)S(1)}, f32[1,256,128]{1,2,0:T(8,128)}, f32[1,256,128]{1,2,0:T(8,128)}, f32[1,256,128]{1,2,0:T(8,128)}...) while((s32[]{:T(128)}, f32[25,256,128]{1,2,0:T(8,128)S(1)}, f32[1,256,128]{1,2,0:T(8,128)}, ...), condition=%wide.region_8.9_spmd, body=%wide.region_7.8_spmd.sunk | while | flops 20622068 | bytes 69660736 | solution.py:134
  188.3 6.1 collective-permute-start.1
  205.9 5.4 collective-permute-start.3
  217.4 14.4 %pad_maximum_fusion.15 = (f32[25,257,130]{2,1,0:T(8,128)}, f32[25,257,130]{2,1,0:T(8,128)}) fusion(f32[25,1,130]{2,1,0:T(1,128)} %collective-permute-done.2, f32[25,256,1]{2,1,0:T(8,128)} %copy.575, f32[25,256,128]{2,1,0:T(8,128)S(1)} %copy.576, f32[25,256,1]{2,1,0:T(8,128)} %copy.577, f32[25,1,130]{2,1,0:T(1,128)} %collective-permute-done.3), kind=kLoop, calls=%fused_computation.9.clone.1 | loop fusion | flops 5011500 | bytes 10036000 | tf_op jit(solution)/shard_map/while/body/eval_jaxpr/concatenate | solution.py:15
  231.8 17.5 %fusion.42 = f32[25,256,128]{2,1,0:T(8,128)} fusion(f32[25,257,130]{2,1,0:T(8,128)} %get-tuple-element.196, f32[25,257,130]{2,1,0:T(8,128)} %get-tuple-element.197, f32[25,256,128]{2,1,0:T(8,128)S(1)} %copy.576, f32[25,256,1]{2,1,0:T(8,128)} %copy.577, f32[25,256,1]{2,1,0:T(8,128)} %copy.575, f32[256,128]{1,0:T(8,128)S(1)} %copy.578, ...), kind=kLoop, calls=%fused_computation.13.clone.1 | loop fusion | flops 15564800 | bytes 26920960 | tf_op jit(solution)/shard_map/while/body/eval_jaxpr/add | solution.py:56
  266.4 5.2 collective-permute-start.3
  277.7 14.4 %pad_maximum_fusion.15 = (f32[25,257,130]{2,1,0:T(8,128)}, f32[25,257,130]{2,1,0:T(8,128)}) fusion(f32[25,1,130]{2,1,0:T(1,128)} %collective-permute-done.2, f32[25,256,1]{2,1,0:T(8,128)} %copy.575, f32[25,256,128]{2,1,0:T(8,128)S(1)} %copy.576, f32[25,256,1]{2,1,0:T(8,128)} %copy.577, f32[25,1,130]{2,1,0:T(1,128)} %collective-permute-done.3), kind=kLoop, calls=%fused_computation.9.clone.1 | loop fusion | flops 5011500 | bytes 10036000 | tf_op jit(solution)/shard_map/while/body/eval_jaxpr/concatenate | solution.py:15
  292.1 17.5 %fusion.42 = f32[25,256,128]{2,1,0:T(8,128)} fusion(f32[25,257,130]{2,1,0:T(8,128)} %get-tuple-element.196, f32[25,257,130]{2,1,0:T(8,128)} %get-tuple-element.197, f32[25,256,128]{2,1,0:T(8,128)S(1)} %copy.576, f32[25,256,1]{2,1,0:T(8,128)} %copy.577, f32[25,256,1]{2,1,0:T(8,128)} %copy.575, f32[256,128]{1,0:T(8,128)S(1)} %copy.578, ...), kind=kLoop, calls=%fused_computation.13.clone.1 | loop fusion | flops 15564800 | bytes 26920960 | tf_op jit(solution)/shard_map/while/body/eval_jaxpr/add | solution.py:56
  315.2 3.7 copy.576
  326.7 5.2 collective-permute-start.3
  338.0 14.4 %pad_maximum_fusion.15 = (f32[25,257,130]{2,1,0:T(8,128)}, f32[25,257,130]{2,1,0:T(8,128)}) fusion(f32[25,1,130]{2,1,0:T(1,128)} %collective-permute-done.2, f32[25,256,1]{2,1,0:T(8,128)} %copy.575, f32[25,256,128]{2,1,0:T(8,128)S(1)} %copy.576, f32[25,256,1]{2,1,0:T(8,128)} %copy.577, f32[25,1,130]{2,1,0:T(1,128)} %collective-permute-done.3), kind=kLoop, calls=%fused_computation.9.clone.1 | loop fusion | flops 5011500 | bytes 10036000 | tf_op jit(solution)/shard_map/while/body/eval_jaxpr/concatenate | solution.py:15
  352.3 17.5 %fusion.42 = f32[25,256,128]{2,1,0:T(8,128)} fusion(f32[25,257,130]{2,1,0:T(8,128)} %get-tuple-element.196, f32[25,257,130]{2,1,0:T(8,128)} %get-tuple-element.197, f32[25,256,128]{2,1,0:T(8,128)S(1)} %copy.576, f32[25,256,1]{2,1,0:T(8,128)} %copy.577, f32[25,256,1]{2,1,0:T(8,128)} %copy.575, f32[256,128]{1,0:T(8,128)S(1)} %copy.578, ...), kind=kLoop, calls=%fused_computation.13.clone.1 | loop fusion | flops 15564800 | bytes 26920960 | tf_op jit(solution)/shard_map/while/body/eval_jaxpr/add | solution.py:56
  376.4 3.7 copy.576
  387.9 4.6 collective-permute-start.3
  398.6 14.4 %pad_maximum_fusion.15 = (f32[25,257,130]{2,1,0:T(8,128)}, f32[25,257,130]{2,1,0:T(8,128)}) fusion(f32[25,1,130]{2,1,0:T(1,128)} %collective-permute-done.2, f32[25,256,1]{2,1,0:T(8,128)} %copy.575, f32[25,256,128]{2,1,0:T(8,128)S(1)} %copy.576, f32[25,256,1]{2,1,0:T(8,128)} %copy.577, f32[25,1,130]{2,1,0:T(1,128)} %collective-permute-done.3), kind=kLoop, calls=%fused_computation.9.clone.1 | loop fusion | flops 5011500 | bytes 10036000 | tf_op jit(solution)/shard_map/while/body/eval_jaxpr/concatenate | solution.py:15
  413.0 17.5 %fusion.42 = f32[25,256,128]{2,1,0:T(8,128)} fusion(f32[25,257,130]{2,1,0:T(8,128)} %get-tuple-element.196, f32[25,257,130]{2,1,0:T(8,128)} %get-tuple-element.197, f32[25,256,128]{2,1,0:T(8,128)S(1)} %copy.576, f32[25,256,1]{2,1,0:T(8,128)} %copy.577, f32[25,256,1]{2,1,0:T(8,128)} %copy.575, f32[256,128]{1,0:T(8,128)S(1)} %copy.578, ...), kind=kLoop, calls=%fused_computation.13.clone.1 | loop fusion | flops 15564800 | bytes 26920960 | tf_op jit(solution)/shard_map/while/body/eval_jaxpr/add | solution.py:56
  434.2 5.7 collective-permute-start
  439.9 3.7 copy.576
  451.4 4.6 collective-permute-start.3
  462.1 14.4 %pad_maximum_fusion.15 = (f32[25,257,130]{2,1,0:T(8,128)}, f32[25,257,130]{2,1,0:T(8,128)}) fusion(f32[25,1,130]{2,1,0:T(1,128)} %collective-permute-done.2, f32[25,256,1]{2,1,0:T(8,128)} %copy.575, f32[25,256,128]{2,1,0:T(8,128)S(1)} %copy.576, f32[25,256,1]{2,1,0:T(8,128)} %copy.577, f32[25,1,130]{2,1,0:T(1,128)} %collective-permute-done.3), kind=kLoop, calls=%fused_computation.9.clone.1 | loop fusion | flops 5011500 | bytes 10036000 | tf_op jit(solution)/shard_map/while/body/eval_jaxpr/concatenate | solution.py:15
  476.5 17.5 %fusion.42 = f32[25,256,128]{2,1,0:T(8,128)} fusion(f32[25,257,130]{2,1,0:T(8,128)} %get-tuple-element.196, f32[25,257,130]{2,1,0:T(8,128)} %get-tuple-element.197, f32[25,256,128]{2,1,0:T(8,128)S(1)} %copy.576, f32[25,256,1]{2,1,0:T(8,128)} %copy.577, f32[25,256,1]{2,1,0:T(8,128)} %copy.575, f32[256,128]{1,0:T(8,128)S(1)} %copy.578, ...), kind=kLoop, calls=%fused_computation.13.clone.1 | loop fusion | flops 15564800 | bytes 26920960 | tf_op jit(solution)/shard_map/while/body/eval_jaxpr/add | solution.py:56
  497.7 5.7 collective-permute-start
  503.4 3.7 copy.576
  514.9 4.6 collective-permute-start.3
  525.6 14.4 %pad_maximum_fusion.15 = (f32[25,257,130]{2,1,0:T(8,128)}, f32[25,257,130]{2,1,0:T(8,128)}) fusion(f32[25,1,130]{2,1,0:T(1,128)} %collective-permute-done.2, f32[25,256,1]{2,1,0:T(8,128)} %copy.575, f32[25,256,128]{2,1,0:T(8,128)S(1)} %copy.576, f32[25,256,1]{2,1,0:T(8,128)} %copy.577, f32[25,1,130]{2,1,0:T(1,128)} %collective-permute-done.3), kind=kLoop, calls=%fused_computation.9.clone.1 | loop fusion | flops 5011500 | bytes 10036000 | tf_op jit(solution)/shard_map/while/body/eval_jaxpr/concatenate | solution.py:15
  540.0 17.5 %fusion.42 = f32[25,256,128]{2,1,0:T(8,128)} fusion(f32[25,257,130]{2,1,0:T(8,128)} %get-tuple-element.196, f32[25,257,130]{2,1,0:T(8,128)} %get-tuple-element.197, f32[25,256,128]{2,1,0:T(8,128)S(1)} %copy.576, f32[25,256,1]{2,1,0:T(8,128)} %copy.577, f32[25,256,1]{2,1,0:T(8,128)} %copy.575, f32[256,128]{1,0:T(8,128)S(1)} %copy.578, ...), kind=kLoop, calls=%fused_computation.13.clone.1 | loop fusion | flops 15564800 | bytes 26920960 | tf_op jit(solution)/shard_map/while/body/eval_jaxpr/add | solution.py:56
  561.2 5.7 collective-permute-start
  566.9 3.7 copy.576
  578.4 4.6 collective-permute-start.3
  589.1 14.4 %pad_maximum_fusion.15 = (f32[25,257,130]{2,1,0:T(8,128)}, f32[25,257,130]{2,1,0:T(8,128)}) fusion(f32[25,1,130]{2,1,0:T(1,128)} %collective-permute-done.2, f32[25,256,1]{2,1,0:T(8,128)} %copy.575, f32[25,256,128]{2,1,0:T(8,128)S(1)} %copy.576, f32[25,256,1]{2,1,0:T(8,128)} %copy.577, f32[25,1,130]{2,1,0:T(1,128)} %collective-permute-done.3), kind=kLoop, calls=%fused_computation.9.clone.1 | loop fusion | flops 5011500 | bytes 10036000 | tf_op jit(solution)/shard_map/while/body/eval_jaxpr/concatenate | solution.py:15
  603.5 17.5 %fusion.42 = f32[25,256,128]{2,1,0:T(8,128)} fusion(f32[25,257,130]{2,1,0:T(8,128)} %get-tuple-element.196, f32[25,257,130]{2,1,0:T(8,128)} %get-tuple-element.197, f32[25,256,128]{2,1,0:T(8,128)S(1)} %copy.576, f32[25,256,1]{2,1,0:T(8,128)} %copy.577, f32[25,256,1]{2,1,0:T(8,128)} %copy.575, f32[256,128]{1,0:T(8,128)S(1)} %copy.578, ...), kind=kLoop, calls=%fused_computation.13.clone.1 | loop fusion | flops 15564800 | bytes 26920960 | tf_op jit(solution)/shard_map/while/body/eval_jaxpr/add | solution.py:56
  624.7 5.7 collective-permute-start
  630.4 3.7 copy.576
  641.9 4.6 collective-permute-start.3
  652.6 14.4 %pad_maximum_fusion.15 = (f32[25,257,130]{2,1,0:T(8,128)}, f32[25,257,130]{2,1,0:T(8,128)}) fusion(f32[25,1,130]{2,1,0:T(1,128)} %collective-permute-done.2, f32[25,256,1]{2,1,0:T(8,128)} %copy.575, f32[25,256,128]{2,1,0:T(8,128)S(1)} %copy.576, f32[25,256,1]{2,1,0:T(8,128)} %copy.577, f32[25,1,130]{2,1,0:T(1,128)} %collective-permute-done.3), kind=kLoop, calls=%fused_computation.9.clone.1 | loop fusion | flops 5011500 | bytes 10036000 | tf_op jit(solution)/shard_map/while/body/eval_jaxpr/concatenate | solution.py:15
  667.0 17.5 %fusion.42 = f32[25,256,128]{2,1,0:T(8,128)} fusion(f32[25,257,130]{2,1,0:T(8,128)} %get-tuple-element.196, f32[25,257,130]{2,1,0:T(8,128)} %get-tuple-element.197, f32[25,256,128]{2,1,0:T(8,128)S(1)} %copy.576, f32[25,256,1]{2,1,0:T(8,128)} %copy.577, f32[25,256,1]{2,1,0:T(8,128)} %copy.575, f32[256,128]{1,0:T(8,128)S(1)} %copy.578, ...), kind=kLoop, calls=%fused_computation.13.clone.1 | loop fusion | flops 15564800 | bytes 26920960 | tf_op jit(solution)/shard_map/while/body/eval_jaxpr/add | solution.py:56
  688.2 5.7 collective-permute-start
  693.9 3.7 copy.576
  705.4 4.6 collective-permute-start.3
  716.2 14.4 %pad_maximum_fusion.15 = (f32[25,257,130]{2,1,0:T(8,128)}, f32[25,257,130]{2,1,0:T(8,128)}) fusion(f32[25,1,130]{2,1,0:T(1,128)} %collective-permute-done.2, f32[25,256,1]{2,1,0:T(8,128)} %copy.575, f32[25,256,128]{2,1,0:T(8,128)S(1)} %copy.576, f32[25,256,1]{2,1,0:T(8,128)} %copy.577, f32[25,1,130]{2,1,0:T(1,128)} %collective-permute-done.3), kind=kLoop, calls=%fused_computation.9.clone.1 | loop fusion | flops 5011500 | bytes 10036000 | tf_op jit(solution)/shard_map/while/body/eval_jaxpr/concatenate | solution.py:15
  730.5 17.5 %fusion.42 = f32[25,256,128]{2,1,0:T(8,128)} fusion(f32[25,257,130]{2,1,0:T(8,128)} %get-tuple-element.196, f32[25,257,130]{2,1,0:T(8,128)} %get-tuple-element.197, f32[25,256,128]{2,1,0:T(8,128)S(1)} %copy.576, f32[25,256,1]{2,1,0:T(8,128)} %copy.577, f32[25,256,1]{2,1,0:T(8,128)} %copy.575, f32[256,128]{1,0:T(8,128)S(1)} %copy.578, ...), kind=kLoop, calls=%fused_computation.13.clone.1 | loop fusion | flops 15564800 | bytes 26920960 | tf_op jit(solution)/shard_map/while/body/eval_jaxpr/add | solution.py:56
  751.7 5.7 collective-permute-start
  757.4 3.7 copy.576
  768.9 4.6 collective-permute-start.3
  779.7 14.4 %pad_maximum_fusion.15 = (f32[25,257,130]{2,1,0:T(8,128)}, f32[25,257,130]{2,1,0:T(8,128)}) fusion(f32[25,1,130]{2,1,0:T(1,128)} %collective-permute-done.2, f32[25,256,1]{2,1,0:T(8,128)} %copy.575, f32[25,256,128]{2,1,0:T(8,128)S(1)} %copy.576, f32[25,256,1]{2,1,0:T(8,128)} %copy.577, f32[25,1,130]{2,1,0:T(1,128)} %collective-permute-done.3), kind=kLoop, calls=%fused_computation.9.clone.1 | loop fusion | flops 5011500 | bytes 10036000 | tf_op jit(solution)/shard_map/while/body/eval_jaxpr/concatenate | solution.py:15
  794.0 17.5 %fusion.42 = f32[25,256,128]{2,1,0:T(8,128)} fusion(f32[25,257,130]{2,1,0:T(8,128)} %get-tuple-element.196, f32[25,257,130]{2,1,0:T(8,128)} %get-tuple-element.197, f32[25,256,128]{2,1,0:T(8,128)S(1)} %copy.576, f32[25,256,1]{2,1,0:T(8,128)} %copy.577, f32[25,256,1]{2,1,0:T(8,128)} %copy.575, f32[256,128]{1,0:T(8,128)S(1)} %copy.578, ...), kind=kLoop, calls=%fused_computation.13.clone.1 | loop fusion | flops 15564800 | bytes 26920960 | tf_op jit(solution)/shard_map/while/body/eval_jaxpr/add | solution.py:56
  821.5 9.0 %copy.564 = f32[25,256,128]{0,2,1:T(8,128)} copy(f32[25,256,128]{2,1,0:T(8,128)S(1)} %mul.199) | data formatting | bytes 6553600 | tf_op jit(solution)/shard_map/mul | solution.py:135
  830.6 8.6 gather_fusion
  839.2 8.6 gather_fusion.1
  847.8 8.6 gather_fusion.2
  856.3 8.8 gather_fusion.3
  867.7 21.8 %all_to_all.37 = f32[128,1,200]{2,1,0:T(1,128)S(1)} all-to-all(f32[128,1,200]{2,1,0:T(1,128)S(1)} %reshape.483), channel_id=1, replica_groups=mesh['lat'=8,'lon'=16] {'lat','lon'}, dimensions={0} | all-to-all | bytes 204800 | tf_op jit(solution)/shard_map/all_to_all | solution.py:144
  (505 shorter events, 242.9 us)
Async XLA Ops:
  0.7 23.1 %copy-start.28 = (s32[512]{0:T(512)S(1)}, s32[512]{0:T(512)}, u32[]{:S(2)}) copy-start(s32[512]{0:T(512)} %param.16) | copy-start | bytes 6148
  0.7 23.1 %copy-start.27 = (s32[512]{0:T(512)S(1)}, s32[512]{0:T(512)}, u32[]{:S(2)}) copy-start(s32[512]{0:T(512)} %param.17) | copy-start | bytes 6148
  5.5 67.9 %collective-permute-start.4 = (f32[4,256,2]{1,2,0:T(2,128)}, f32[4,256,2]{1,2,0:T(2,128)S(1)}, u32[]{:S(2)}, u32[]{:S(2)}) collective-permute-start(f32[4,256,2]{1,2,0:T(2,128)} %get-tuple-element.109), channel_id=1, source_target_pairs={{0,1},{1,2},{2,3},{3,4},{4,5},{5,6},{6,7},{7,8},{8,9},{9,10},{10,1... | collective-permute-start | bytes 24584 | tf_op jit(solution)/shard_map/ppermute | solution.py:17
  8.5 64.9 %collective-permute-start.5 = (f32[4,256,2]{1,2,0:T(2,128)}, f32[4,256,2]{1,2,0:T(2,128)S(1)}, u32[]{:S(2)}, u32[]{:S(2)}) collective-permute-start(f32[4,256,2]{1,2,0:T(2,128)} %get-tuple-element.110), channel_id=1, source_target_pairs={{1,0},{2,1},{3,2},{4,3},{5,4},{6,5},{7,6},{8,7},{9,8},{10,9},{11,1... | collective-permute-start | bytes 24584 | tf_op jit(solution)/shard_map/ppermute | solution.py:19
  10.9 23.2 %all-to-all-start.2 = ((s32[1,16,2]{2,0,1:T(1,128)}), s32[1,16,2]{2,0,1:T(1,128)}, u32[]{:S(2)}, u32[]{:S(2)}) async-start(s32[1,16,2]{2,0,1:T(1,128)} %bitcast.19), calls=%async_computation.2 | async-start | bytes 16384 | tf_op jit(solution)/shard_map/all_to_all | solution.py:86
  34.1 19.0 %all-to-all-start = ((s32[1,128,8]{2,0,1:T(1,128)}), s32[1,128,8]{2,0,1:T(1,128)S(1)}, u32[]{:S(2)}, u32[]{:S(2)}) async-start(s32[1,128,8]{2,0,1:T(1,128)} %bitcast.635), calls=%async_computation | async-start | bytes 131072 | tf_op jit(solution)/shard_map/all_to_all | solution.py:108
  53.2 14.4 %all-to-all-start.1 = ((f32[128,1,232]{2,1,0:T(1,128)}), f32[128,1,232]{2,1,0:T(1,128)S(1)}, u32[]{:S(2)}, u32[]{:S(2)}) async-start(f32[128,1,232]{2,1,0:T(1,128)} %reshape.481), calls=%async_computation.1 | async-start | bytes 262144 | tf_op jit(solution)/shard_map/all_to_all | solution.py:107
  67.6 105.4 %all-to-all-start.3 = ((f32[25,32,8,128]{3,2,0,1:T(8,128)}), f32[25,32,8,128]{3,2,0,1:T(8,128)}, u32[]{:S(2)}, u32[]{:S(2)}) async-start(f32[25,32,8,128]{3,2,0,1:T(8,128)} %copy.555), calls=%async_computation.3 | async-start | bytes 6553600 | tf_op jit(solution)/shard_map/all_to_all | solution.py:85
  73.6 48.7 %collective-permute-start.6 = (f32[4,2,132]{1,2,0:T(8,128)S(1)}, f32[4,2,132]{1,2,0:T(8,128)S(1)}, u32[]{:S(2)}, u32[]{:S(2)}) collective-permute-start(f32[4,2,132]{1,2,0:T(8,128)S(1)} %get-tuple-element.107), channel_id=1, source_target_pairs={{0,16},{16,32},{32,48},{48,64},{64,80},{80,96},{96,112},{1,17},{17... | collective-permute-start | bytes 12680 | tf_op jit(solution)/shard_map/ppermute | solution.py:17
  75.9 46.4 %collective-permute-start.7 = (f32[4,2,132]{1,2,0:T(8,128)S(1)}, f32[4,2,132]{1,2,0:T(8,128)S(1)}, u32[]{:S(2)}, u32[]{:S(2)}) collective-permute-start(f32[4,2,132]{1,2,0:T(8,128)S(1)} %get-tuple-element.108), channel_id=1, source_target_pairs={{16,0},{32,16},{48,32},{64,48},{80,64},{96,80},{112,96},{17,1},{33... | collective-permute-start | bytes 12680 | tf_op jit(solution)/shard_map/ppermute | solution.py:19
  186.6 24.7 %copy-start.3 = (f32[1,256,128]{1,2,0:T(8,128)}, f32[1,256,128]{1,2,0:T(8,128)S(1)}, u32[]{:S(2)}) copy-start(f32[1,256,128]{1,2,0:T(8,128)S(1)} %get-tuple-element.220) | copy-start | bytes 393220 | tf_op jit(solution)/shard_map/while
  186.7 11.5 %collective-permute-start = (f32[25,256,1]{1,2,0:T(1,128)S(1)}, f32[25,256,1]{1,2,0:T(1,128)S(1)}, u32[]{:S(2)}, u32[]{:S(2)}) collective-permute-start(f32[25,256,1]{1,2,0:T(1,128)S(1)} %get-tuple-element.192), channel_id=1, source_target_pairs={{1,0},{2,1},{3,2},{4,3},{5,4},{6,5},{7,6},{8,7},{9,8},{10,9},{11,1... | collective-permute-start | bytes 76808 | tf_op jit(solution)/shard_map/while/body/eval_jaxpr/ppermute | solution.py:19
  188.3 12.1 %collective-permute-start.1 = (f32[25,256,1]{1,2,0:T(1,128)S(1)}, f32[25,256,1]{1,2,0:T(1,128)S(1)}, u32[]{:S(2)}, u32[]{:S(2)}) collective-permute-start(f32[25,256,1]{1,2,0:T(1,128)S(1)} %get-tuple-element.193), channel_id=1, source_target_pairs={{0,1},{1,2},{2,3},{3,4},{4,5},{5,6},{6,7},{7,8},{8,9},{9,10},{10,1... | collective-permute-start | bytes 76808 | tf_op jit(solution)/shard_map/while/body/eval_jaxpr/ppermute | solution.py:17
  204.6 12.8 %collective-permute-start.2 = (f32[25,1,130]{2,1,0:T(1,128)}, f32[25,1,130]{2,1,0:T(1,128)}, u32[]{:S(2)}, u32[]{:S(2)}) collective-permute-start(f32[25,1,130]{2,1,0:T(1,128)} %get-tuple-element.194), channel_id=1, source_target_pairs={{16,0},{32,16},{48,32},{64,48},{80,64},{96,80},{112,96},{17,1},{33... | collective-permute-start | bytes 39008 | tf_op jit(solution)/shard_map/while/body/eval_jaxpr/ppermute | solution.py:19
  205.9 11.5 %collective-permute-start.3 = (f32[25,1,130]{2,1,0:T(1,128)}, f32[25,1,130]{2,1,0:T(1,128)}, u32[]{:S(2)}, u32[]{:S(2)}) collective-permute-start(f32[25,1,130]{2,1,0:T(1,128)} %get-tuple-element.195), channel_id=1, source_target_pairs={{0,16},{16,32},{32,48},{48,64},{64,80},{80,96},{96,112},{1,17},{17... | collective-permute-start | bytes 39008 | tf_op jit(solution)/shard_map/while/body/eval_jaxpr/ppermute | solution.py:17
  253.0 5.6 collective-permute-start
  254.6 6.3 collective-permute-start.1
  265.1 12.6 %collective-permute-start.2 = (f32[25,1,130]{2,1,0:T(1,128)}, f32[25,1,130]{2,1,0:T(1,128)}, u32[]{:S(2)}, u32[]{:S(2)}) collective-permute-start(f32[25,1,130]{2,1,0:T(1,128)} %get-tuple-element.194), channel_id=1, source_target_pairs={{16,0},{32,16},{48,32},{64,48},{80,64},{96,80},{112,96},{17,1},{33... | collective-permute-start | bytes 39008 | tf_op jit(solution)/shard_map/while/body/eval_jaxpr/ppermute | solution.py:19
  266.4 11.3 %collective-permute-start.3 = (f32[25,1,130]{2,1,0:T(1,128)}, f32[25,1,130]{2,1,0:T(1,128)}, u32[]{:S(2)}, u32[]{:S(2)}) collective-permute-start(f32[25,1,130]{2,1,0:T(1,128)} %get-tuple-element.195), channel_id=1, source_target_pairs={{0,16},{16,32},{32,48},{48,64},{64,80},{80,96},{96,112},{1,17},{17... | collective-permute-start | bytes 39008 | tf_op jit(solution)/shard_map/while/body/eval_jaxpr/ppermute | solution.py:17
  313.3 5.6 collective-permute-start
  314.9 6.3 collective-permute-start.1
  325.4 12.6 %collective-permute-start.2 = (f32[25,1,130]{2,1,0:T(1,128)}, f32[25,1,130]{2,1,0:T(1,128)}, u32[]{:S(2)}, u32[]{:S(2)}) collective-permute-start(f32[25,1,130]{2,1,0:T(1,128)} %get-tuple-element.194), channel_id=1, source_target_pairs={{16,0},{32,16},{48,32},{64,48},{80,64},{96,80},{112,96},{17,1},{33... | collective-permute-start | bytes 39008 | tf_op jit(solution)/shard_map/while/body/eval_jaxpr/ppermute | solution.py:19
  326.7 11.3 %collective-permute-start.3 = (f32[25,1,130]{2,1,0:T(1,128)}, f32[25,1,130]{2,1,0:T(1,128)}, u32[]{:S(2)}, u32[]{:S(2)}) collective-permute-start(f32[25,1,130]{2,1,0:T(1,128)} %get-tuple-element.195), channel_id=1, source_target_pairs={{0,16},{16,32},{32,48},{48,64},{64,80},{80,96},{96,112},{1,17},{17... | collective-permute-start | bytes 39008 | tf_op jit(solution)/shard_map/while/body/eval_jaxpr/ppermute | solution.py:17
  373.5 6.5 collective-permute-start
  376.4 6.0 collective-permute-start.1
  386.6 12.0 %collective-permute-start.2 = (f32[25,1,130]{2,1,0:T(1,128)}, f32[25,1,130]{2,1,0:T(1,128)}, u32[]{:S(2)}, u32[]{:S(2)}) collective-permute-start(f32[25,1,130]{2,1,0:T(1,128)} %get-tuple-element.194), channel_id=1, source_target_pairs={{16,0},{32,16},{48,32},{64,48},{80,64},{96,80},{112,96},{17,1},{33... | collective-permute-start | bytes 39008 | tf_op jit(solution)/shard_map/while/body/eval_jaxpr/ppermute | solution.py:19
  387.9 10.7 %collective-permute-start.3 = (f32[25,1,130]{2,1,0:T(1,128)}, f32[25,1,130]{2,1,0:T(1,128)}, u32[]{:S(2)}, u32[]{:S(2)}) collective-permute-start(f32[25,1,130]{2,1,0:T(1,128)} %get-tuple-element.195), channel_id=1, source_target_pairs={{0,16},{16,32},{32,48},{48,64},{64,80},{80,96},{96,112},{1,17},{17... | collective-permute-start | bytes 39008 | tf_op jit(solution)/shard_map/while/body/eval_jaxpr/ppermute | solution.py:17
  434.1 21.9 %copy-start.3 = (f32[1,256,128]{1,2,0:T(8,128)}, f32[1,256,128]{1,2,0:T(8,128)S(1)}, u32[]{:S(2)}) copy-start(f32[1,256,128]{1,2,0:T(8,128)S(1)} %get-tuple-element.220) | copy-start | bytes 393220 | tf_op jit(solution)/shard_map/while
  434.2 9.4 %collective-permute-start = (f32[25,256,1]{1,2,0:T(1,128)S(1)}, f32[25,256,1]{1,2,0:T(1,128)S(1)}, u32[]{:S(2)}, u32[]{:S(2)}) collective-permute-start(f32[25,256,1]{1,2,0:T(1,128)S(1)} %get-tuple-element.192), channel_id=1, source_target_pairs={{1,0},{2,1},{3,2},{4,3},{5,4},{6,5},{7,6},{8,7},{9,8},{10,9},{11,1... | collective-permute-start | bytes 76808 | tf_op jit(solution)/shard_map/while/body/eval_jaxpr/ppermute | solution.py:19
  439.9 6.0 collective-permute-start.1
  450.1 12.0 %collective-permute-start.2 = (f32[25,1,130]{2,1,0:T(1,128)}, f32[25,1,130]{2,1,0:T(1,128)}, u32[]{:S(2)}, u32[]{:S(2)}) collective-permute-start(f32[25,1,130]{2,1,0:T(1,128)} %get-tuple-element.194), channel_id=1, source_target_pairs={{16,0},{32,16},{48,32},{64,48},{80,64},{96,80},{112,96},{17,1},{33... | collective-permute-start | bytes 39008 | tf_op jit(solution)/shard_map/while/body/eval_jaxpr/ppermute | solution.py:19
  451.4 10.7 %collective-permute-start.3 = (f32[25,1,130]{2,1,0:T(1,128)}, f32[25,1,130]{2,1,0:T(1,128)}, u32[]{:S(2)}, u32[]{:S(2)}) collective-permute-start(f32[25,1,130]{2,1,0:T(1,128)} %get-tuple-element.195), channel_id=1, source_target_pairs={{0,16},{16,32},{32,48},{48,64},{64,80},{80,96},{96,112},{1,17},{17... | collective-permute-start | bytes 39008 | tf_op jit(solution)/shard_map/while/body/eval_jaxpr/ppermute | solution.py:17
  497.6 21.9 %copy-start.3 = (f32[1,256,128]{1,2,0:T(8,128)}, f32[1,256,128]{1,2,0:T(8,128)S(1)}, u32[]{:S(2)}) copy-start(f32[1,256,128]{1,2,0:T(8,128)S(1)} %get-tuple-element.220) | copy-start | bytes 393220 | tf_op jit(solution)/shard_map/while
  497.7 9.4 %collective-permute-start = (f32[25,256,1]{1,2,0:T(1,128)S(1)}, f32[25,256,1]{1,2,0:T(1,128)S(1)}, u32[]{:S(2)}, u32[]{:S(2)}) collective-permute-start(f32[25,256,1]{1,2,0:T(1,128)S(1)} %get-tuple-element.192), channel_id=1, source_target_pairs={{1,0},{2,1},{3,2},{4,3},{5,4},{6,5},{7,6},{8,7},{9,8},{10,9},{11,1... | collective-permute-start | bytes 76808 | tf_op jit(solution)/shard_map/while/body/eval_jaxpr/ppermute | solution.py:19
  503.4 6.0 collective-permute-start.1
  513.6 12.0 %collective-permute-start.2 = (f32[25,1,130]{2,1,0:T(1,128)}, f32[25,1,130]{2,1,0:T(1,128)}, u32[]{:S(2)}, u32[]{:S(2)}) collective-permute-start(f32[25,1,130]{2,1,0:T(1,128)} %get-tuple-element.194), channel_id=1, source_target_pairs={{16,0},{32,16},{48,32},{64,48},{80,64},{96,80},{112,96},{17,1},{33... | collective-permute-start | bytes 39008 | tf_op jit(solution)/shard_map/while/body/eval_jaxpr/ppermute | solution.py:19
  514.9 10.7 %collective-permute-start.3 = (f32[25,1,130]{2,1,0:T(1,128)}, f32[25,1,130]{2,1,0:T(1,128)}, u32[]{:S(2)}, u32[]{:S(2)}) collective-permute-start(f32[25,1,130]{2,1,0:T(1,128)} %get-tuple-element.195), channel_id=1, source_target_pairs={{0,16},{16,32},{32,48},{48,64},{64,80},{80,96},{96,112},{1,17},{17... | collective-permute-start | bytes 39008 | tf_op jit(solution)/shard_map/while/body/eval_jaxpr/ppermute | solution.py:17
  561.1 21.9 %copy-start.3 = (f32[1,256,128]{1,2,0:T(8,128)}, f32[1,256,128]{1,2,0:T(8,128)S(1)}, u32[]{:S(2)}) copy-start(f32[1,256,128]{1,2,0:T(8,128)S(1)} %get-tuple-element.220) | copy-start | bytes 393220 | tf_op jit(solution)/shard_map/while
  561.2 9.4 %collective-permute-start = (f32[25,256,1]{1,2,0:T(1,128)S(1)}, f32[25,256,1]{1,2,0:T(1,128)S(1)}, u32[]{:S(2)}, u32[]{:S(2)}) collective-permute-start(f32[25,256,1]{1,2,0:T(1,128)S(1)} %get-tuple-element.192), channel_id=1, source_target_pairs={{1,0},{2,1},{3,2},{4,3},{5,4},{6,5},{7,6},{8,7},{9,8},{10,9},{11,1... | collective-permute-start | bytes 76808 | tf_op jit(solution)/shard_map/while/body/eval_jaxpr/ppermute | solution.py:19
  566.9 6.0 collective-permute-start.1
  577.1 12.0 %collective-permute-start.2 = (f32[25,1,130]{2,1,0:T(1,128)}, f32[25,1,130]{2,1,0:T(1,128)}, u32[]{:S(2)}, u32[]{:S(2)}) collective-permute-start(f32[25,1,130]{2,1,0:T(1,128)} %get-tuple-element.194), channel_id=1, source_target_pairs={{16,0},{32,16},{48,32},{64,48},{80,64},{96,80},{112,96},{17,1},{33... | collective-permute-start | bytes 39008 | tf_op jit(solution)/shard_map/while/body/eval_jaxpr/ppermute | solution.py:19
  578.4 10.7 %collective-permute-start.3 = (f32[25,1,130]{2,1,0:T(1,128)}, f32[25,1,130]{2,1,0:T(1,128)}, u32[]{:S(2)}, u32[]{:S(2)}) collective-permute-start(f32[25,1,130]{2,1,0:T(1,128)} %get-tuple-element.195), channel_id=1, source_target_pairs={{0,16},{16,32},{32,48},{48,64},{64,80},{80,96},{96,112},{1,17},{17... | collective-permute-start | bytes 39008 | tf_op jit(solution)/shard_map/while/body/eval_jaxpr/ppermute | solution.py:17
  624.6 21.9 %copy-start.3 = (f32[1,256,128]{1,2,0:T(8,128)}, f32[1,256,128]{1,2,0:T(8,128)S(1)}, u32[]{:S(2)}) copy-start(f32[1,256,128]{1,2,0:T(8,128)S(1)} %get-tuple-element.220) | copy-start | bytes 393220 | tf_op jit(solution)/shard_map/while
  624.7 9.4 %collective-permute-start = (f32[25,256,1]{1,2,0:T(1,128)S(1)}, f32[25,256,1]{1,2,0:T(1,128)S(1)}, u32[]{:S(2)}, u32[]{:S(2)}) collective-permute-start(f32[25,256,1]{1,2,0:T(1,128)S(1)} %get-tuple-element.192), channel_id=1, source_target_pairs={{1,0},{2,1},{3,2},{4,3},{5,4},{6,5},{7,6},{8,7},{9,8},{10,9},{11,1... | collective-permute-start | bytes 76808 | tf_op jit(solution)/shard_map/while/body/eval_jaxpr/ppermute | solution.py:19
  630.4 6.0 collective-permute-start.1
  640.6 12.0 %collective-permute-start.2 = (f32[25,1,130]{2,1,0:T(1,128)}, f32[25,1,130]{2,1,0:T(1,128)}, u32[]{:S(2)}, u32[]{:S(2)}) collective-permute-start(f32[25,1,130]{2,1,0:T(1,128)} %get-tuple-element.194), channel_id=1, source_target_pairs={{16,0},{32,16},{48,32},{64,48},{80,64},{96,80},{112,96},{17,1},{33... | collective-permute-start | bytes 39008 | tf_op jit(solution)/shard_map/while/body/eval_jaxpr/ppermute | solution.py:19
  641.9 10.7 %collective-permute-start.3 = (f32[25,1,130]{2,1,0:T(1,128)}, f32[25,1,130]{2,1,0:T(1,128)}, u32[]{:S(2)}, u32[]{:S(2)}) collective-permute-start(f32[25,1,130]{2,1,0:T(1,128)} %get-tuple-element.195), channel_id=1, source_target_pairs={{0,16},{16,32},{32,48},{48,64},{64,80},{80,96},{96,112},{1,17},{17... | collective-permute-start | bytes 39008 | tf_op jit(solution)/shard_map/while/body/eval_jaxpr/ppermute | solution.py:17
  688.2 21.9 %copy-start.3 = (f32[1,256,128]{1,2,0:T(8,128)}, f32[1,256,128]{1,2,0:T(8,128)S(1)}, u32[]{:S(2)}) copy-start(f32[1,256,128]{1,2,0:T(8,128)S(1)} %get-tuple-element.220) | copy-start | bytes 393220 | tf_op jit(solution)/shard_map/while
  688.2 9.4 %collective-permute-start = (f32[25,256,1]{1,2,0:T(1,128)S(1)}, f32[25,256,1]{1,2,0:T(1,128)S(1)}, u32[]{:S(2)}, u32[]{:S(2)}) collective-permute-start(f32[25,256,1]{1,2,0:T(1,128)S(1)} %get-tuple-element.192), channel_id=1, source_target_pairs={{1,0},{2,1},{3,2},{4,3},{5,4},{6,5},{7,6},{8,7},{9,8},{10,9},{11,1... | collective-permute-start | bytes 76808 | tf_op jit(solution)/shard_map/while/body/eval_jaxpr/ppermute | solution.py:19
  693.9 6.0 collective-permute-start.1
  704.1 12.0 %collective-permute-start.2 = (f32[25,1,130]{2,1,0:T(1,128)}, f32[25,1,130]{2,1,0:T(1,128)}, u32[]{:S(2)}, u32[]{:S(2)}) collective-permute-start(f32[25,1,130]{2,1,0:T(1,128)} %get-tuple-element.194), channel_id=1, source_target_pairs={{16,0},{32,16},{48,32},{64,48},{80,64},{96,80},{112,96},{17,1},{33... | collective-permute-start | bytes 39008 | tf_op jit(solution)/shard_map/while/body/eval_jaxpr/ppermute | solution.py:19
  705.4 10.7 %collective-permute-start.3 = (f32[25,1,130]{2,1,0:T(1,128)}, f32[25,1,130]{2,1,0:T(1,128)}, u32[]{:S(2)}, u32[]{:S(2)}) collective-permute-start(f32[25,1,130]{2,1,0:T(1,128)} %get-tuple-element.195), channel_id=1, source_target_pairs={{0,16},{16,32},{32,48},{48,64},{64,80},{80,96},{96,112},{1,17},{17... | collective-permute-start | bytes 39008 | tf_op jit(solution)/shard_map/while/body/eval_jaxpr/ppermute | solution.py:17
  751.7 21.9 %copy-start.3 = (f32[1,256,128]{1,2,0:T(8,128)}, f32[1,256,128]{1,2,0:T(8,128)S(1)}, u32[]{:S(2)}) copy-start(f32[1,256,128]{1,2,0:T(8,128)S(1)} %get-tuple-element.220) | copy-start | bytes 393220 | tf_op jit(solution)/shard_map/while
  751.7 9.4 %collective-permute-start = (f32[25,256,1]{1,2,0:T(1,128)S(1)}, f32[25,256,1]{1,2,0:T(1,128)S(1)}, u32[]{:S(2)}, u32[]{:S(2)}) collective-permute-start(f32[25,256,1]{1,2,0:T(1,128)S(1)} %get-tuple-element.192), channel_id=1, source_target_pairs={{1,0},{2,1},{3,2},{4,3},{5,4},{6,5},{7,6},{8,7},{9,8},{10,9},{11,1... | collective-permute-start | bytes 76808 | tf_op jit(solution)/shard_map/while/body/eval_jaxpr/ppermute | solution.py:19
  757.4 6.0 collective-permute-start.1
  767.6 12.0 %collective-permute-start.2 = (f32[25,1,130]{2,1,0:T(1,128)}, f32[25,1,130]{2,1,0:T(1,128)}, u32[]{:S(2)}, u32[]{:S(2)}) collective-permute-start(f32[25,1,130]{2,1,0:T(1,128)} %get-tuple-element.194), channel_id=1, source_target_pairs={{16,0},{32,16},{48,32},{64,48},{80,64},{96,80},{112,96},{17,1},{33... | collective-permute-start | bytes 39008 | tf_op jit(solution)/shard_map/while/body/eval_jaxpr/ppermute | solution.py:19
  768.9 10.7 %collective-permute-start.3 = (f32[25,1,130]{2,1,0:T(1,128)}, f32[25,1,130]{2,1,0:T(1,128)}, u32[]{:S(2)}, u32[]{:S(2)}) collective-permute-start(f32[25,1,130]{2,1,0:T(1,128)} %get-tuple-element.195), channel_id=1, source_target_pairs={{0,16},{16,32},{32,48},{48,64},{64,80},{80,96},{96,112},{1,17},{17... | collective-permute-start | bytes 39008 | tf_op jit(solution)/shard_map/while/body/eval_jaxpr/ppermute | solution.py:17
  821.5 26.3 %copy-start.21 = (s32[1024]{0:T(1024)S(1)}, s32[1024]{0:T(1024)}, u32[]{:S(2)}) copy-start(s32[1024]{0:T(1024)} %get-tuple-element.141) | copy-start | bytes 12292
  830.5 25.8 %copy-start.19 = (s32[1024]{0:T(1024)S(1)}, s32[1024]{0:T(1024)}, u32[]{:S(2)}) copy-start(s32[1024]{0:T(1024)} %get-tuple-element.140) | copy-start | bytes 12292
  830.5 34.6 %copy-start.11 = (f32[1024]{0:T(1024)S(1)}, f32[1024]{0:T(1024)}, u32[]{:S(2)}) copy-start(f32[1024]{0:T(1024)} %copy-done.10) | copy-start | bytes 12292
  830.5 34.7 %copy-start.13 = (f32[1024]{0:T(1024)S(1)}, f32[1024]{0:T(1024)}, u32[]{:S(2)}) copy-start(f32[1024]{0:T(1024)} %copy-done.12) | copy-start | bytes 12292
  830.5 34.7 %copy-start.15 = (f32[1024]{0:T(1024)S(1)}, f32[1024]{0:T(1024)}, u32[]{:S(2)}) copy-start(f32[1024]{0:T(1024)} %copy-done.14) | copy-start | bytes 12292
  830.6 34.7 %copy-start.17 = (f32[1024]{0:T(1024)S(1)}, f32[1024]{0:T(1024)}, u32[]{:S(2)}) copy-start(f32[1024]{0:T(1024)} %copy-done.16) | copy-start | bytes 12292
  865.2 25.5 %copy-start.23 = (s32[1024]{0:T(1024)S(1)}, s32[1024]{0:T(1024)}, u32[]{:S(2)}) copy-start(s32[1024]{0:T(1024)} %get-tuple-element.139) | copy-start | bytes 12292
  (41 other events, 325.0 us)
